TPU v7x, 32 devices: a whole 2x2x4 slice. The times are simulated.
32 devices in a mesh: row: 4 (over z), col: 8 (over y, x, core).
Axes of the slice: x: 2, y: 2, z: 4, core: 2. Of those that a mesh axis runs over, the one named last changes fastest.
Arguments:
- scene_tokens: bfloat16 [64, 512, 180], P('row', 'col'), may hold values from -8 to 8
- block_qkv: bfloat16 [3, 180, 540], replicated, may hold values from -1.8 to 1.8
- block_proj: bfloat16 [3, 180, 180], replicated, may hold values from -0.4375 to 0.4375
- conv_squeeze: bfloat16 [3, 9, 180, 60], replicated, may hold values from -0.15625 to 0.15625
- conv_expand: bfloat16 [3, 9, 60, 180], replicated, may hold values from -0.25 to 0.25
- gate_down: bfloat16 [3, 180, 6], replicated, may hold values from -4 to 4
- gate_up: bfloat16 [3, 6, 180], replicated, may hold values from -6 to 6
- mlp_in: bfloat16 [4, 180, 360], replicated, may hold values from -0.4375 to 0.4375
- mlp_out: bfloat16 [4, 360, 180], replicated, may hold values from -0.3125 to 0.3125
- ocab_qkv: bfloat16 [180, 540], replicated, may hold values from -1.8 to 1.8
- ocab_proj: bfloat16 [180, 180], replicated, may hold values from -0.4375 to 0.4375
Outputs:
- refined: bfloat16 [64, 512, 180], P('row', 'col')
All inputs are finite; a program needn't handle non-finite values.
Results may differ from a plain program's by a relative error of at most 0.034.
Values may be sent and summed in bfloat16 or wider, within the bound.
No kernel may reach another device: no remote copies, remote signals or barrier semaphores. Data moves between devices by JAX's collectives and lax.ppermute only.
A program may use at most 128 MiB of HBM per device.

v0:
```python
import functools

import jax
import jax.numpy as jnp
from jax import lax
from jax.experimental import pallas as pl
from jax.experimental.pallas import tpu as pltpu
from jax.sharding import PartitionSpec as P

C = 180
HEADS = 6
HEAD = 30
WIN = 16
HID = 360
CC = 60
CP = 64
SHIFT = 8
OVL = 4
EDGE = 8
EPSILON = 1e-05
MASKED = -1000000000.0
BF16 = jnp.bfloat16
F32 = jnp.float32


def dot(a, b):
    return jnp.dot(a, b, preferred_element_type=F32)


def dot_nt(a, b):
    return lax.dot_general(a, b, (((1,), (1,)), ((), ())), preferred_element_type=F32)


def layer_norm(x):
    middle = jnp.sum(x, axis=-1, keepdims=True) * (1.0 / C)
    centered = x - middle
    spread = jnp.sum(centered * centered, axis=-1, keepdims=True) * (1.0 / C)
    return (centered * lax.rsqrt(spread + EPSILON)).astype(BF16)


def gelu(v):
    return v * (lax.erf(v * (0.5**0.5)) + 1.0) * 0.5


def head_masks(rows):
    lane = lax.broadcasted_iota(jnp.int32, (rows, C), 1)
    return [(lane >= HEAD * h) & (lane < HEAD * (h + 1)) for h in range(HEADS)]


def attend(q, k, v, bias):
    n, m = q.shape[0], k.shape[0]
    q_masks = head_masks(n)
    v_masks = head_masks(m)
    zero_q = jnp.zeros_like(q)
    zero_v = jnp.zeros_like(v)
    one_v = jnp.ones_like(v)
    top = jnp.zeros((n, C), F32)
    bottom = jnp.zeros((n, C), F32)
    for h in range(HEADS):
        scores = dot_nt(jnp.where(q_masks[h], q, zero_q), k) * HEAD ** (-0.5)
        if bias is not None:
            scores = scores + bias
        highest = jnp.max(scores, axis=-1, keepdims=True)
        powers = jnp.exp(scores - highest).astype(BF16)
        top = top + dot(powers, jnp.where(v_masks[h], v, zero_v))
        bottom = bottom + dot(powers, jnp.where(v_masks[h], one_v, zero_v))
    return (top / bottom).astype(BF16)


def norm_kernel(x_ref, u_ref):
    u_ref[...] = layer_norm(x_ref[...].astype(F32))


def window_kernel(u_ref, qkv_ref, proj_ref, out_ref):
    w = qkv_ref[...]
    wq, wk, wv = w[:, :C], w[:, C : 2 * C], w[:, 2 * C :]
    proj = proj_ref[...]
    height, breadth = u_ref.shape[0], u_ref.shape[1]
    for i in range(height // WIN):

        def body(j, carry):
            cols = pl.ds(pl.multiple_of(j * WIN, WIN), WIN)
            rows = pl.ds(i * WIN, WIN)
            u = u_ref[rows, cols, :].reshape(WIN * WIN, C)
            q = dot(u, wq).astype(BF16)
            k = dot(u, wk).astype(BF16)
            v = dot(u, wv).astype(BF16)
            heads = attend(q, k, v, None)
            out_ref[rows, cols, :] = dot(heads, proj).reshape(WIN, WIN, C)
            return carry

        lax.fori_loop(0, breadth // WIN, body, 0)


def place(ext, flags_ref, u_ref, row_e, row_o, col_e, col_o, width, left, convert):
    height, breadth = u_ref.shape[0], u_ref.shape[1]
    row_odd = flags_ref[0] == 1
    col_odd = flags_ref[1] == 1
    inside = [flags_ref[2 + s] == 1 for s in range(4)]

    def pick(cond, a, b, keep):
        value = jnp.where(cond, a[...].astype(F32), b[...].astype(F32))
        return convert(jnp.where(keep, value, 0.0))

    ext[width : width + height, left : left + breadth, :] = convert(u_ref[...].astype(F32))
    ext[0:width, left : left + breadth, :] = pick(row_odd, row_e, row_o, inside[0])
    ext[width + height :, left : left + breadth, :] = pick(row_odd, row_o, row_e, inside[1])
    tall = height + 2 * width
    west = pick(col_odd, col_e, col_o, inside[2])
    east = pick(col_odd, col_o, col_e, inside[3])
    rows_at = lax.broadcasted_iota(jnp.int32, (tall, 1, 1), 0)
    real = ((rows_at >= width) | inside[0]) & ((rows_at < width + height) | inside[1])
    west = jnp.where(real, west.astype(F32), 0.0).astype(west.dtype)
    east = jnp.where(real, east.astype(F32), 0.0).astype(east.dtype)
    side = col_e.shape[1]
    ext[0:tall, left - side : left, :] = west
    ext[0:tall, left + breadth : left + breadth + side, :] = east


def shifted_kernel(
    flags_ref, u_ref, row_e, row_o, col_e, col_o, qkv_ref, proj_ref, out_ref, ext, wide
):
    height, breadth = u_ref.shape[0], u_ref.shape[1]
    place(ext, flags_ref, u_ref, row_e, row_o, col_e, col_o, SHIFT, SHIFT, lambda x: x)
    w = qkv_ref[...]
    wq, wk, wv = w[:, :C], w[:, C : 2 * C], w[:, 2 * C :]
    proj = proj_ref[...]
    north, south, west, east = [flags_ref[2 + s] == 1 for s in range(4)]
    count_i = height // WIN + 1
    count_j = breadth // WIN + 1
    key = lax.broadcasted_iota(jnp.int32, (1, WIN * WIN), 1)
    key_row, key_col = key // WIN, key % WIN
    for i in range(count_i):
        low = SHIFT if i == 0 else 0
        high = SHIFT if i == count_i - 1 else WIN

        def body(j, carry):
            cols = pl.ds(pl.multiple_of(j * WIN, WIN), WIN)
            u = ext[i * WIN : (i + 1) * WIN, cols, :]
            part = u[low:high].reshape((high - low) * WIN, C).astype(BF16)
            u = u.reshape(WIN * WIN, C).astype(BF16)
            bad = jnp.zeros((1, WIN * WIN), jnp.bool_)
            if i == 0:
                bad = bad | ((key_row < SHIFT) & jnp.logical_not(north))
            if i == count_i - 1:
                bad = bad | ((key_row >= SHIFT) & jnp.logical_not(south))
            bad = bad | ((key_col < SHIFT) & (jnp.logical_not(west) & (j == 0)))
            bad = bad | ((key_col >= SHIFT) & (jnp.logical_not(east) & (j == count_j - 1)))
            bias = jnp.where(bad, MASKED, 0.0)
            q = dot(part, wq).astype(BF16)
            k = dot(u, wk).astype(BF16)
            v = dot(u, wv).astype(BF16)
            heads = attend(q, k, v, bias)
            wide[i * WIN + low - SHIFT : i * WIN + high - SHIFT, cols, :] = dot(
                heads, proj
            ).reshape(high - low, WIN, C)
            return carry

        lax.fori_loop(0, count_j, body, 0)
    out_ref[...] = wide[:, SHIFT : SHIFT + breadth, :]


def cross_kernel(
    flags_ref, u_ref, row_e, row_o, col_e, col_o, qkv_ref, proj_ref, out_ref, ext, keys, values
):
    height, breadth = u_ref.shape[0], u_ref.shape[1]
    place(ext, flags_ref, u_ref, row_e, row_o, col_e, col_o, OVL, EDGE, lambda x: x)
    w = qkv_ref[...]
    wq, wk, wv = w[:, :C], w[:, C : 2 * C], w[:, 2 * C :]
    proj = proj_ref[...]
    tall, long = ext.shape[0], ext.shape[1]
    side = WIN + 2 * OVL
    flat = pltpu.roll(ext[...].reshape(tall * long, C), tall * long - (EDGE - OVL), 0)
    flat = flat.astype(BF16)
    keys[...] = dot(flat, wk).astype(BF16).astype(F32).reshape(tall, long, C)
    values[...] = dot(flat, wv).astype(BF16).astype(F32).reshape(tall, long, C)
    for i in range(height // WIN):

        def body(j, carry):
            at = j * WIN
            rows = pl.ds(i * WIN, WIN)
            u = u_ref[rows, pl.ds(at, WIN), :].reshape(WIN * WIN, C)
            q = dot(u, wq).astype(BF16)
            area = (pl.ds(i * WIN, side), pl.ds(at, side), slice(None))
            k = keys[area].reshape(side * side, C).astype(BF16)
            v = values[area].reshape(side * side, C).astype(BF16)
            heads = attend(q, k, v, None)
            out_ref[rows, pl.ds(at, WIN), :] = dot(heads, proj).reshape(WIN, WIN, C)
            return carry

        for j in range(breadth // WIN):
            body(j, 0)


def conv_kernel(
    width, flags_ref, u_ref, row_e, row_o, col_e, col_o, w1_ref, w2_ref, out_ref, sum_ref, ext, hid
):
    height, breadth = u_ref.shape[0], u_ref.shape[1]
    pitch = breadth + 2 * EDGE
    grid = ext.at[...]
    place(grid, flags_ref, u_ref, row_e, row_o, col_e, col_o, width, EDGE, lambda x: x)
    north, south, west, east = [flags_ref[2 + s] == 1 for s in range(4)]
    tall = height + 4
    first = width - 2
    flat = ext[first : first + tall].reshape(tall * pitch, C)
    acc = None
    for b in range(3):
        moved = flat if b == 1 else pltpu.roll(flat, (1 - b) % (tall * pitch), 0)
        part = dot(moved.astype(BF16), w1_ref[b])
        acc = part if acc is None else acc + part
    acc = acc.reshape(tall, pitch, 3 * CP)
    rows = height + 2
    pre = (
        acc[0:rows, :, 0:CP]
        + acc[1 : rows + 1, :, CP : 2 * CP]
        + acc[2 : rows + 2, :, 2 * CP : 3 * CP]
    )
    hidden = gelu(pre)
    row_at = lax.broadcasted_iota(jnp.int32, (rows, pitch, CP), 0)
    col_at = lax.broadcasted_iota(jnp.int32, (rows, pitch, CP), 1)
    real = ((row_at >= 1) | north) & ((row_at < rows - 1) | south)
    real = real & (col_at >= jnp.where(west, EDGE - 1, EDGE))
    real = real & (col_at < EDGE + breadth + jnp.where(east, 1, 0))
    hidden = jnp.where(real, hidden, 0.0).reshape(rows * pitch, CP)
    total = rows * pitch
    three = jnp.concatenate(
        [
            pltpu.roll(hidden, 1, 0),
            hidden,
            pltpu.roll(hidden, total - 1, 0),
        ],
        axis=1,
    ).astype(BF16)
    out = None
    for a in range(3):
        part = dot(three[a * pitch : (a + height) * pitch], w2_ref[a])
        out = part if out is None else out + part
    out = out.reshape(height, pitch, C)[:, EDGE : EDGE + breadth, :]
    out_ref[...] = out
    sums = jnp.sum(jnp.sum(out, axis=0), axis=0, keepdims=True)
    for i in range(sum_ref.shape[0]):
        sum_ref[i] = sums


def ff_tail(x, in_ref, out_w_ref):
    hidden = gelu(dot(layer_norm(x), in_ref[...])).astype(BF16)
    return x + dot(hidden, out_w_ref[...])


def block_kernel(
    rim, area, flags_ref, x_ref, att_ref, exp_ref, sums_ref, down_ref, up_ref, in_ref, out_w_ref,
    y_ref, u_ref, even_ref, odd_ref,
):
    pooled = jnp.sum(sums_ref[...], axis=0) * (1.0 / area)
    squeezed = jnp.sum(down_ref[...] * pooled, axis=-1, keepdims=True)
    squeezed = jnp.maximum(squeezed, 0.0)
    gate = jax.nn.sigmoid(jnp.sum(up_ref[...] * squeezed, axis=0, keepdims=True))
    height, breadth = x_ref.shape[0], x_ref.shape[1]
    step = 4

    def body(r, carry):
        rows = pl.ds(r * step, step)
        x = x_ref[rows].reshape(step * breadth, C).astype(F32)
        x = x + att_ref[rows].reshape(step * breadth, C)
        x = x + exp_ref[rows].reshape(step * breadth, C) * gate
        y = ff_tail(x, in_ref, out_w_ref)
        y_ref[rows] = y.reshape(step, breadth, C)
        u_ref[rows] = layer_norm(y).reshape(step, breadth, C)
        return carry

    lax.fori_loop(0, height // step, body, 0)
    rims(rim, flags_ref, u_ref, even_ref, odd_ref)


def rims(rim, flags_ref, u_ref, even_ref, odd_ref):
    height = u_ref.shape[0]
    head = u_ref[0:rim]
    tail = u_ref[height - rim :]
    odd = flags_ref[0] == 1

    @pl.when(odd)
    def _():
        even_ref[...] = head
        odd_ref[...] = tail

    @pl.when(jnp.logical_not(odd))
    def _():
        even_ref[...] = tail
        odd_ref[...] = head


def first_kernel(rim, flags_ref, x_ref, u_ref, even_ref, odd_ref):
    u_ref[...] = layer_norm(x_ref[...].astype(F32))
    rims(rim, flags_ref, u_ref, even_ref, odd_ref)


def last_kernel(x_ref, att_ref, in_ref, out_w_ref, y_ref):
    height, breadth = x_ref.shape[0], x_ref.shape[1]
    step = 4

    def body(r, carry):
        rows = pl.ds(r * step, step)
        x = (x_ref[rows] + att_ref[rows]).reshape(step * breadth, C)
        y = ff_tail(x, in_ref, out_w_ref)
        y_ref[rows] = y.astype(BF16).reshape(step, breadth, C)
        return carry

    lax.fori_loop(0, height // step, body, 0)


VM = pl.BlockSpec(memory_space=pltpu.VMEM)
SM = pl.BlockSpec(memory_space=pltpu.SMEM)


def call(kernel, name, outs, scratch, flags, *args):
    specs = [VM] * len(args)
    if flags is not None:
        specs = [SM] + specs
        args = (flags,) + args
    return pl.pallas_call(
        kernel,
        out_shape=outs,
        in_specs=specs,
        out_specs=jax.tree.map(lambda _: VM, outs),
        scratch_shapes=scratch,
        name=name,
        compiler_params=pltpu.CompilerParams(vmem_limit_bytes=48 * 1024 * 1024),
    )(*args)


def swap(value, axis, odd):
    count = lax.axis_size(axis)
    pairs = []
    for i in range(count):
        step = 1 if (i % 2 == 0) != odd else -1
        pairs.append((i, (i + step) % count))
    return lax.ppermute(value, axis, pairs)


def exchange(u, even, odd, width, side, flags):
    row_e = swap(even, "row", False)
    row_o = swap(odd, "row", True)
    row_odd = flags[0] == 1
    col_odd = flags[1] == 1
    above = jnp.where(row_odd, row_e, row_o)
    below = jnp.where(row_odd, row_o, row_e)
    breadth = u.shape[1]
    head = jnp.concatenate([a[:, :side] for a in (above, u, below)], axis=0)
    tail = jnp.concatenate([a[:, breadth - side :] for a in (above, u, below)], axis=0)
    col_e = swap(jnp.where(col_odd, head, tail), "col", False)
    col_o = swap(jnp.where(col_odd, tail, head), "col", True)
    return row_e, row_o, col_e, col_o


def local(
    scene_tokens, block_qkv, block_proj, conv_squeeze, conv_expand, gate_down, gate_up,
    mlp_in, mlp_out, ocab_qkv, ocab_proj,
):
    height, breadth = scene_tokens.shape[0], scene_tokens.shape[1]
    row_count, col_count = lax.axis_size("row"), lax.axis_size("col")
    area = height * row_count * breadth * col_count
    devices = row_count * col_count
    row, col = lax.axis_index("row"), lax.axis_index("col")
    flags = jnp.stack(
        [
            row % 2,
            col % 2,
            (row > 0).astype(jnp.int32),
            (row < row_count - 1).astype(jnp.int32),
            (col > 0).astype(jnp.int32),
            (col < col_count - 1).astype(jnp.int32),
        ]
    ).astype(jnp.int32)
    w1 = conv_squeeze.reshape(3, 3, 3, C, CC).transpose(0, 2, 3, 1, 4)
    w1 = jnp.pad(w1, ((0, 0), (0, 0), (0, 0), (0, 0), (0, CP - CC))).reshape(3, 3, C, 3 * CP)
    w2 = jnp.pad(conv_expand, ((0, 0), (0, 0), (0, CP - CC), (0, 0))).reshape(3, 3, 3 * CP, C)
    down = gate_down.transpose(0, 2, 1).astype(F32)
    up = gate_up.astype(F32)

    def shape(rows, cols, dtype):
        return jax.ShapeDtypeStruct((rows, cols, C), dtype)

    tile = shape(height, breadth, F32)
    tile16 = shape(height, breadth, BF16)
    widths = [2, SHIFT, 2, OVL]

    def rim_shape(k):
        return shape(widths[k], breadth, BF16)

    u, even, odd = call(
        functools.partial(first_kernel, widths[0]), "norm",
        (tile16, rim_shape(0), rim_shape(0)), [], flags, scene_tokens,
    )
    stream = scene_tokens
    for k in range(3):
        width = widths[k]
        halo = exchange(u, even, odd, width, width, flags)
        if k == 1:
            tall, long = height + 2 * SHIFT, breadth + 2 * SHIFT
            att = call(
                shifted_kernel, "shifted_attention", tile,
                [pltpu.VMEM((tall, long, C), F32), pltpu.VMEM((height, long, C), F32)],
                flags, u, *halo, block_qkv[k], block_proj[k],
            )
        else:
            att = call(window_kernel, "window_attention", tile, [], None, u, block_qkv[k], block_proj[k])
        pitch = breadth + 2 * EDGE
        expanded, sums = call(
            functools.partial(conv_kernel, width), "convolutions",
            (tile, jax.ShapeDtypeStruct((devices, 1, C), F32)),
            [pltpu.VMEM((height + 2 * width, pitch, C), F32), pltpu.VMEM((8, 128), F32)],
            flags, u, *halo, w1[k], w2[k],
        )
        sums = lax.all_to_all(sums, ("row", "col"), 0, 0)
        stream, u, even, odd = call(
            functools.partial(block_kernel, widths[k + 1], area), "feed_forward",
            (tile, tile16, rim_shape(k + 1), rim_shape(k + 1)), [],
            flags, stream, att, expanded, sums, down[k], up[k], mlp_in[k], mlp_out[k],
        )
    halo = exchange(u, even, odd, OVL, EDGE, flags)
    tall, long = height + 2 * OVL, breadth + 2 * EDGE
    att = call(
        cross_kernel, "cross_attention", tile,
        [pltpu.VMEM((tall, long, C), F32)] * 3,
        flags, u, *halo, ocab_qkv, ocab_proj,
    )
    return call(last_kernel, "last", tile16, [], None, stream, att, mlp_in[3], mlp_out[3])


def solution(mesh):
    return jax.shard_map(
        local,
        mesh=mesh,
        in_specs=(P("row", "col", None),) + (P(),) * 10,
        out_specs=P("row", "col", None),
        check_vma=False,
    )
```

profile of v0, /device:TPU:0, one launch (start us, length us, event | category | flops | bytes accessed | tf_op | source)
XLA Modules:
  0.0 175.5 jit_solution(13010689212773518890)
XLA Ops:
  0.1 1.0 copy-done
  2.1 3.1 %collective-permute-start = (bf16[2,64,180]{2,1,0:T(8,128)(2,1)S(1)}, bf16[2,64,180]{2,1,0:T(8,128)(2,1)S(1)}, u32[]{:S(2)}, u32[]{:S(2)}) collective-permute-start(bf16[2,64,180]{2,1,0:T(8,128)(2,1)S(1)} %get-tuple-element.27), channel_id=1, source_target_pairs={{0,8},{8,0},{16,24},{24,16},{1,9},{9,1},{17,25},{25,17},{2,10},{10... | collective-permute-start | bytes 138248 | tf_op jit(solution)/shard_map/ppermute | solution.py:337
  5.2 2.5 %collective-permute-start.1 = (bf16[2,64,180]{2,1,0:T(8,128)(2,1)S(1)}, bf16[2,64,180]{2,1,0:T(8,128)(2,1)S(1)}, u32[]{:S(2)}, u32[]{:S(2)}) collective-permute-start(bf16[2,64,180]{2,1,0:T(8,128)(2,1)S(1)} %get-tuple-element.28), channel_id=1, source_target_pairs={{0,24},{8,16},{16,8},{24,0},{1,25},{9,17},{17,9},{25,1},{2,26},{10... | collective-permute-start | bytes 138248 | tf_op jit(solution)/shard_map/ppermute | solution.py:337
  7.7 1.8 %slice_bitcast_fusion.3 = (bf16[180,180]{1,0:T(8,128)(2,1)}, bf16[180,180]{1,0:T(8,128)(2,1)}, bf16[180,180]{1,0:T(8,128)(2,1)}) fusion(bf16[3,180,180]{2,1,0:T(8,128)(2,1)} %param.13), kind=kLoop, calls=%fused_computation.26 | loop fusion | bytes 388800 | tf_op jit(solution)/shard_map/squeeze | solution.py:406
  10.4 1.0 copy-done.24
  11.4 1.7 fusion.1
  13.0 1.7 fusion
  14.7 1.0 pad_slice_fusion.3
  15.9 1.4 collective-permute-start.3
  17.5 1.3 pad_slice_fusion
  19.0 1.1 collective-permute-done.3.col_o
  20.2 3.7 %convolutions.3 = (f32[16,64,180]{2,1,0:T(8,128)S(1)}, f32[32,1,180]{2,1,0:T(1,128)}) custom-call(s32[6]{0:T(128)S(1)} %stack.43.flags_ref, bf16[16,64,180]{2,1,0:T(8,128)(2,1)S(1)} %get-tuple-element.26.u_ref, bf16[2,64,180]{2,1,0:T(8,128)(2,1)S(1)} %collective-permute-done.row_e, bf16[2,64,180]{2,1,0:T(8,128)(2,1)S(1)} %collective-permute-done.1.row_o, ...), custom_call_target="tpu_custom_call" | custom-call | tf_op jit(solution)/shard_map/convolutions/pallas_call | solution.py:320
  24.8 2.6 %all-to-all-start = ((f32[32,1,180]{2,1,0:T(1,128)}), f32[32,1,180]{2,1,0:T(1,128)S(1)}, u32[]{:S(2)}, u32[]{:S(2)}) async-start(f32[32,1,180]{2,1,0:T(1,128)} %get-tuple-element.30), calls=%async_computation | async-start | bytes 65536 | tf_op jit(solution)/shard_map/all_to_all | solution.py:414
  29.1 8.5 %window_attention.2.att_ref = f32[16,64,180]{2,1,0:T(8,128)S(1)} custom-call(bf16[16,64,180]{2,1,0:T(8,128)(2,1)S(1)} %get-tuple-element.26.u_ref, bf16[180,540]{1,0:T(8,128)(2,1)S(1)} %get-tuple-element.54.qkv_ref, bf16[180,180]{1,0:T(8,128)(2,1)S(1)} %copy-done.18), custom_call_target="tpu_custom_call" | custom-call | tf_op jit(solution)/shard_map/window_attention/pallas_call | solution.py:320
  38.3 1.2 copy-done.3
  40.3 3.6 %feed_forward.3 = (f32[16,64,180]{2,1,0:T(8,128)S(1)}, bf16[16,64,180]{2,1,0:T(8,128)(2,1)S(1)}, bf16[8,64,180]{2,1,0:T(8,128)(2,1)S(1)}, bf16[8,64,180]{2,1,0:T(8,128)(2,1)S(1)}) custom-call(s32[6]{0:T(128)S(1)} %stack.43.flags_ref, bf16[16,64,180]{2,1,0:T(8,128)(2,1)S(1)} %copy-done.1, f32[16,64,180]{2,1,0:T(8,128)S(1)} %window_attention.2.att_ref, ...), custom_call_target="tpu_custom_call" | custom-call | tf_op jit(solution)/shard_map/feed_forward/pallas_call | solution.py:320
  43.9 1.8 %collective-permute-start.4 = (bf16[8,64,180]{2,1,0:T(8,128)(2,1)S(1)}, bf16[8,64,180]{2,1,0:T(8,128)(2,1)S(1)}, u32[]{:S(2)}, u32[]{:S(2)}) collective-permute-start(bf16[8,64,180]{2,1,0:T(8,128)(2,1)S(1)} %get-tuple-element.33), channel_id=1, source_target_pairs={{0,8},{8,0},{16,24},{24,16},{1,9},{9,1},{17,25},{25,17},{2,10},{10... | collective-permute-start | bytes 552968 | tf_op jit(solution)/shard_map/ppermute | solution.py:337
  45.7 2.4 %collective-permute-start.5 = (bf16[8,64,180]{2,1,0:T(8,128)(2,1)S(1)}, bf16[8,64,180]{2,1,0:T(8,128)(2,1)S(1)}, u32[]{:S(2)}, u32[]{:S(2)}) collective-permute-start(bf16[8,64,180]{2,1,0:T(8,128)(2,1)S(1)} %get-tuple-element.34), channel_id=1, source_target_pairs={{0,24},{8,16},{16,8},{24,0},{1,25},{9,17},{17,9},{25,1},{2,26},{10... | collective-permute-start | bytes 552968 | tf_op jit(solution)/shard_map/ppermute | solution.py:337
  48.1 4.3 %collective-permute-done.4.row_e = bf16[8,64,180]{2,1,0:T(8,128)(2,1)S(1)} collective-permute-done((bf16[8,64,180]{2,1,0:T(8,128)(2,1)S(1)}, bf16[8,64,180]{2,1,0:T(8,128)(2,1)S(1)}, u32[]{:S(2)}, u32[]{:S(2)}) %collective-permute-start.4) | collective-permute-done | bytes 184352 | tf_op jit(solution)/shard_map/ppermute | solution.py:337
  52.4 7.7 %collective-permute-done.5.row_o = bf16[8,64,180]{2,1,0:T(8,128)(2,1)S(1)} collective-permute-done((bf16[8,64,180]{2,1,0:T(8,128)(2,1)S(1)}, bf16[8,64,180]{2,1,0:T(8,128)(2,1)S(1)}, u32[]{:S(2)}, u32[]{:S(2)}) %collective-permute-start.5) | collective-permute-done | bytes 184352 | tf_op jit(solution)/shard_map/ppermute | solution.py:337
  60.2 1.3 collective-permute-start.7
  62.1 4.9 %collective-permute-done.7.col_o = bf16[32,8,180]{2,1,0:T(8,128)(2,1)S(1)} collective-permute-done((bf16[32,8,180]{2,1,0:T(8,128)(2,1)S(1)}, bf16[32,8,180]{2,1,0:T(8,128)(2,1)S(1)}, u32[]{:S(2)}, u32[]{:S(2)}) %collective-permute-start.7) | collective-permute-done | bytes 92192 | tf_op jit(solution)/shard_map/ppermute | solution.py:337
  66.9 3.7 %convolutions.4 = (f32[16,64,180]{2,1,0:T(8,128)S(1)}, f32[32,1,180]{2,1,0:T(1,128)}) custom-call(s32[6]{0:T(128)S(1)} %stack.43.flags_ref, bf16[16,64,180]{2,1,0:T(8,128)(2,1)S(1)} %get-tuple-element.32.u_ref, bf16[8,64,180]{2,1,0:T(8,128)(2,1)S(1)} %collective-permute-done.4.row_e, bf16[8,64,180]{2,1,0:T(8,128)(2,1)S(1)} %collective-permute-done.5.row_o, ...), custom_call_target="tpu_custom_call" | custom-call | tf_op jit(solution)/shard_map/convolutions/pallas_call | solution.py:320
  70.6 1.0 copy-done.8
  71.6 2.9 %all-to-all-start.1 = ((f32[32,1,180]{2,1,0:T(1,128)}), f32[32,1,180]{2,1,0:T(1,128)S(1)}, u32[]{:S(2)}, u32[]{:S(2)}) async-start(f32[32,1,180]{2,1,0:T(1,128)} %get-tuple-element.36), calls=%async_computation.1 | async-start | bytes 65536 | tf_op jit(solution)/shard_map/all_to_all | solution.py:414
  76.1 21.1 %shifted_attention.1.att_ref = f32[16,64,180]{2,1,0:T(8,128)S(1)} custom-call(s32[6]{0:T(128)S(1)} %stack.43.flags_ref, bf16[16,64,180]{2,1,0:T(8,128)(2,1)S(1)} %get-tuple-element.32.u_ref, bf16[8,64,180]{2,1,0:T(8,128)(2,1)S(1)} %collective-permute-done.4.row_e, bf16[8,64,180]{2,1,0:T(8,128)(2,1)S(1)} %collective-permute-done.5.row_o, ...), custom_call_target="tpu_custom_call" | custom-call | tf_op jit(solution)/shard_map/shifted_attention/pallas_call | solution.py:320
  97.9 1.2 copy-done.5
  99.1 1.2 copy-done.9
  102.2 3.6 %feed_forward.4 = (f32[16,64,180]{2,1,0:T(8,128)S(1)}, bf16[16,64,180]{2,1,0:T(8,128)(2,1)S(1)}, bf16[2,64,180]{2,1,0:T(8,128)(2,1)S(1)}, bf16[2,64,180]{2,1,0:T(8,128)(2,1)S(1)}) custom-call(s32[6]{0:T(128)S(1)} %stack.43.flags_ref, f32[16,64,180]{2,1,0:T(8,128)S(1)} %copy-done.5, f32[16,64,180]{2,1,0:T(8,128)S(1)} %shifted_attention.1.att_ref, ...), custom_call_target="tpu_custom_call" | custom-call | tf_op jit(solution)/shard_map/feed_forward/pallas_call | solution.py:320
  105.8 1.6 collective-permute-start.8
  107.3 2.4 %collective-permute-start.9 = (bf16[2,64,180]{2,1,0:T(8,128)(2,1)S(1)}, bf16[2,64,180]{2,1,0:T(8,128)(2,1)S(1)}, u32[]{:S(2)}, u32[]{:S(2)}) collective-permute-start(bf16[2,64,180]{2,1,0:T(8,128)(2,1)S(1)} %get-tuple-element.40), channel_id=1, source_target_pairs={{0,24},{8,16},{16,8},{24,0},{1,25},{9,17},{17,9},{25,1},{2,26},{10... | collective-permute-start | bytes 138248 | tf_op jit(solution)/shard_map/ppermute | solution.py:337
  110.1 3.4 %collective-permute-done.9.row_o = bf16[2,64,180]{2,1,0:T(8,128)(2,1)S(1)} collective-permute-done((bf16[2,64,180]{2,1,0:T(8,128)(2,1)S(1)}, bf16[2,64,180]{2,1,0:T(8,128)(2,1)S(1)}, u32[]{:S(2)}, u32[]{:S(2)}) %collective-permute-start.9) | collective-permute-done | bytes 46112 | tf_op jit(solution)/shard_map/ppermute | solution.py:337
  113.6 1.2 collective-permute-start.11
  115.4 2.5 %collective-permute-done.11.col_o = bf16[20,2,180]{2,1,0:T(2,128)(2,1)S(1)} collective-permute-done((bf16[20,2,180]{2,1,0:T(2,128)(2,1)S(1)}, bf16[20,2,180]{2,1,0:T(2,128)(2,1)S(1)}, u32[]{:S(2)}, u32[]{:S(2)}) %collective-permute-start.11) | collective-permute-done | bytes 14432 | tf_op jit(solution)/shard_map/ppermute | solution.py:337
  117.9 3.7 %convolutions.5 = (f32[16,64,180]{2,1,0:T(8,128)S(1)}, f32[32,1,180]{2,1,0:T(1,128)}) custom-call(s32[6]{0:T(128)S(1)} %stack.43.flags_ref, bf16[16,64,180]{2,1,0:T(8,128)(2,1)S(1)} %get-tuple-element.38.u_ref, bf16[2,64,180]{2,1,0:T(8,128)(2,1)S(1)} %collective-permute-done.8.row_e, bf16[2,64,180]{2,1,0:T(8,128)(2,1)S(1)} %collective-permute-done.9.row_o, ...), custom_call_target="tpu_custom_call" | custom-call | tf_op jit(solution)/shard_map/convolutions/pallas_call | solution.py:320
  121.6 1.0 copy-done.6
  122.6 3.5 %all-to-all-start.2 = ((f32[32,1,180]{2,1,0:T(1,128)}), f32[32,1,180]{2,1,0:T(1,128)S(1)}, u32[]{:S(2)}, u32[]{:S(2)}) async-start(f32[32,1,180]{2,1,0:T(1,128)} %get-tuple-element.42), calls=%async_computation.2 | async-start | bytes 65536 | tf_op jit(solution)/shard_map/all_to_all | solution.py:414
  127.8 8.5 %window_attention.3.att_ref = f32[16,64,180]{2,1,0:T(8,128)S(1)} custom-call(bf16[16,64,180]{2,1,0:T(8,128)(2,1)S(1)} %get-tuple-element.38.u_ref, bf16[180,540]{1,0:T(8,128)(2,1)S(1)} %copy-done.10, bf16[180,180]{1,0:T(8,128)(2,1)S(1)} %copy-done.16), custom_call_target="tpu_custom_call" | custom-call | tf_op jit(solution)/shard_map/window_attention/pallas_call | solution.py:320
  136.3 1.2 copy-done.7
  138.4 3.8 %feed_forward.5 = (f32[16,64,180]{2,1,0:T(8,128)S(1)}, bf16[16,64,180]{2,1,0:T(8,128)(2,1)S(1)}, bf16[4,64,180]{2,1,0:T(8,128)(2,1)S(1)}, bf16[4,64,180]{2,1,0:T(8,128)(2,1)S(1)}) custom-call(s32[6]{0:T(128)S(1)} %stack.43.flags_ref, f32[16,64,180]{2,1,0:T(8,128)S(1)} %get-tuple-element.37.x_ref, f32[16,64,180]{2,1,0:T(8,128)S(1)} %window_attention.3.att_ref, ...), custom_call_target="tpu_custom_call" | custom-call | tf_op jit(solution)/shard_map/feed_forward/pallas_call | solution.py:320
  142.3 1.8 %collective-permute-start.12 = (bf16[4,64,180]{2,1,0:T(8,128)(2,1)S(1)}, bf16[4,64,180]{2,1,0:T(8,128)(2,1)S(1)}, u32[]{:S(2)}, u32[]{:S(2)}) collective-permute-start(bf16[4,64,180]{2,1,0:T(8,128)(2,1)S(1)} %get-tuple-element.45), channel_id=1, source_target_pairs={{0,8},{8,0},{16,24},{24,16},{1,9},{9,1},{17,25},{25,17},{2,10},{10... | collective-permute-start | bytes 276488 | tf_op jit(solution)/shard_map/ppermute | solution.py:337
  144.1 2.4 %collective-permute-start.13 = (bf16[4,64,180]{2,1,0:T(8,128)(2,1)S(1)}, bf16[4,64,180]{2,1,0:T(8,128)(2,1)S(1)}, u32[]{:S(2)}, u32[]{:S(2)}) collective-permute-start(bf16[4,64,180]{2,1,0:T(8,128)(2,1)S(1)} %get-tuple-element.46), channel_id=1, source_target_pairs={{0,24},{8,16},{16,8},{24,0},{1,25},{9,17},{17,9},{25,1},{2,26},{10... | collective-permute-start | bytes 276488 | tf_op jit(solution)/shard_map/ppermute | solution.py:337
  146.5 1.5 collective-permute-done.12.row_e
  148.0 4.8 %collective-permute-done.13.row_o = bf16[4,64,180]{2,1,0:T(8,128)(2,1)S(1)} collective-permute-done((bf16[4,64,180]{2,1,0:T(8,128)(2,1)S(1)}, bf16[4,64,180]{2,1,0:T(8,128)(2,1)S(1)}, u32[]{:S(2)}, u32[]{:S(2)}) %collective-permute-start.13) | collective-permute-done | bytes 92192 | tf_op jit(solution)/shard_map/ppermute | solution.py:337
  153.0 1.3 collective-permute-start.15
  154.9 4.0 %collective-permute-done.15.col_o = bf16[24,8,180]{2,1,0:T(8,128)(2,1)S(1)} collective-permute-done((bf16[24,8,180]{2,1,0:T(8,128)(2,1)S(1)}, bf16[24,8,180]{2,1,0:T(8,128)(2,1)S(1)}, u32[]{:S(2)}, u32[]{:S(2)}) %collective-permute-start.15) | collective-permute-done | bytes 69152 | tf_op jit(solution)/shard_map/ppermute | solution.py:337
  159.0 13.5 %cross_attention.1.att_ref = f32[16,64,180]{2,1,0:T(8,128)S(1)} custom-call(s32[6]{0:T(128)S(1)} %stack.43.flags_ref, bf16[16,64,180]{2,1,0:T(8,128)(2,1)S(1)} %copy-done.12, bf16[4,64,180]{2,1,0:T(8,128)(2,1)S(1)} %collective-permute-done.12.row_e, bf16[4,64,180]{2,1,0:T(8,128)(2,1)S(1)} %collective-permute-done.13.row_o, ...), custom_call_target="tpu_custom_call" | custom-call | tf_op jit(solution)/shard_map/cross_attention/pallas_call | solution.py:320
  172.5 3.0 %last.1 = bf16[16,64,180]{2,1,0:T(8,128)(2,1)} custom-call(f32[16,64,180]{2,1,0:T(8,128)S(1)} %get-tuple-element.43.x_ref, f32[16,64,180]{2,1,0:T(8,128)S(1)} %cross_attention.1.att_ref, bf16[180,360]{1,0:T(8,128)(2,1)S(1)} %bitcast.65, bf16[360,180]{1,0:T(8,128)(2,1)S(1)} %bitcast.62), custom_call_target="tpu_custom_call" | custom-call | tf_op jit(solution)/shard_map/last/pallas_call | solution.py:320
  (119 shorter events, 15.7 us)
Async XLA Ops:
  0.0 7.7 %copy-start.36 = (bf16[3,180,6]{1,2,0:T(8,128)(2,1)S(1)}, bf16[3,180,6]{1,2,0:T(8,128)(2,1)}, u32[]{:S(2)}) copy-start(bf16[3,180,6]{1,2,0:T(8,128)(2,1)} %param.16) | copy-start | bytes 19444
  0.1 1.0 copy-start
  1.1 8.4 %copy-start.35 = (bf16[3,180,540]{2,1,0:T(8,128)(2,1)S(1)}, bf16[3,180,540]{2,1,0:T(8,128)(2,1)}, u32[]{:S(2)}) copy-start(bf16[3,180,540]{2,1,0:T(8,128)(2,1)} %param.12) | copy-start | bytes 1749604
  2.1 13.6 %collective-permute-start = (bf16[2,64,180]{2,1,0:T(8,128)(2,1)S(1)}, bf16[2,64,180]{2,1,0:T(8,128)(2,1)S(1)}, u32[]{:S(2)}, u32[]{:S(2)}) collective-permute-start(bf16[2,64,180]{2,1,0:T(8,128)(2,1)S(1)} %get-tuple-element.27), channel_id=1, source_target_pairs={{0,8},{8,0},{16,24},{24,16},{1,9},{9,1},{17,25},{25,17},{2,10},{10... | collective-permute-start | bytes 138248 | tf_op jit(solution)/shard_map/ppermute | solution.py:337
  5.2 10.5 %collective-permute-start.1 = (bf16[2,64,180]{2,1,0:T(8,128)(2,1)S(1)}, bf16[2,64,180]{2,1,0:T(8,128)(2,1)S(1)}, u32[]{:S(2)}, u32[]{:S(2)}) collective-permute-start(bf16[2,64,180]{2,1,0:T(8,128)(2,1)S(1)} %get-tuple-element.28), channel_id=1, source_target_pairs={{0,24},{8,16},{16,8},{24,0},{1,25},{9,17},{17,9},{25,1},{2,26},{10... | collective-permute-start | bytes 138248 | tf_op jit(solution)/shard_map/ppermute | solution.py:337
  7.7 2.6 %copy-start.34 = (bf16[3,9,180,60]{2,3,1,0:T(8,128)(2,1)S(1)}, bf16[3,9,180,60]{2,3,1,0:T(8,128)(2,1)}, u32[]{:S(2)}) copy-start(bf16[3,9,180,60]{2,3,1,0:T(8,128)(2,1)} %param.14) | copy-start | bytes 1749604
  10.3 1.1 copy-start.24
  11.4 1.7 copy-start.25
  15.9 4.3 %collective-permute-start.3 = (bf16[20,2,180]{2,1,0:T(2,128)(2,1)S(1)}, bf16[20,2,180]{2,1,0:T(2,128)(2,1)S(1)}, u32[]{:S(2)}, u32[]{:S(2)}) collective-permute-start(bf16[20,2,180]{2,1,0:T(2,128)(2,1)S(1)} %get-tuple-element.105), channel_id=1, source_target_pairs={{0,7},{1,2},{2,1},{3,4},{4,3},{5,6},{6,5},{7,0},{8,15},{9,10},{10,... | collective-permute-start | bytes 43208 | tf_op jit(solution)/shard_map/ppermute | solution.py:337
  17.3 1.6 copy-start.37
  17.3 2.9 %collective-permute-start.2 = (bf16[20,2,180]{2,1,0:T(2,128)(2,1)S(1)}, bf16[20,2,180]{2,1,0:T(2,128)(2,1)S(1)}, u32[]{:S(2)}, u32[]{:S(2)}) collective-permute-start(bf16[20,2,180]{2,1,0:T(2,128)(2,1)S(1)} %get-tuple-element.106), channel_id=1, source_target_pairs={{0,1},{1,0},{2,3},{3,2},{4,5},{5,4},{6,7},{7,6},{8,9},{9,8},{10,11... | collective-permute-start | bytes 43208 | tf_op jit(solution)/shard_map/ppermute | solution.py:337
  23.8 1.0 copy-start.2
  24.8 12.8 %all-to-all-start = ((f32[32,1,180]{2,1,0:T(1,128)}), f32[32,1,180]{2,1,0:T(1,128)S(1)}, u32[]{:S(2)}, u32[]{:S(2)}) async-start(f32[32,1,180]{2,1,0:T(1,128)} %get-tuple-element.30), calls=%async_computation | async-start | bytes 65536 | tf_op jit(solution)/shard_map/all_to_all | solution.py:414
  29.1 8.5 %copy-start.1 = (bf16[16,64,180]{2,1,0:T(8,128)(2,1)S(1)}, bf16[16,64,180]{2,1,0:T(8,128)(2,1)}, u32[]{:S(2)}) copy-start(bf16[16,64,180]{2,1,0:T(8,128)(2,1)} %x_ref.3) | copy-start | bytes 1105924
  38.3 1.2 copy-start.3
  43.9 16.3 %copy-start.4 = (f32[16,64,180]{2,1,0:T(8,128)}, f32[16,64,180]{2,1,0:T(8,128)S(1)}, u32[]{:S(2)}) copy-start(f32[16,64,180]{2,1,0:T(8,128)S(1)} %get-tuple-element.31.x_ref) | copy-start | bytes 2211844
  43.9 8.5 %collective-permute-start.4 = (bf16[8,64,180]{2,1,0:T(8,128)(2,1)S(1)}, bf16[8,64,180]{2,1,0:T(8,128)(2,1)S(1)}, u32[]{:S(2)}, u32[]{:S(2)}) collective-permute-start(bf16[8,64,180]{2,1,0:T(8,128)(2,1)S(1)} %get-tuple-element.33), channel_id=1, source_target_pairs={{0,8},{8,0},{16,24},{24,16},{1,9},{9,1},{17,25},{25,17},{2,10},{10... | collective-permute-start | bytes 552968 | tf_op jit(solution)/shard_map/ppermute | solution.py:337
  45.7 14.4 %collective-permute-start.5 = (bf16[8,64,180]{2,1,0:T(8,128)(2,1)S(1)}, bf16[8,64,180]{2,1,0:T(8,128)(2,1)S(1)}, u32[]{:S(2)}, u32[]{:S(2)}) collective-permute-start(bf16[8,64,180]{2,1,0:T(8,128)(2,1)S(1)} %get-tuple-element.34), channel_id=1, source_target_pairs={{0,24},{8,16},{16,8},{24,0},{1,25},{9,17},{17,9},{25,1},{2,26},{10... | collective-permute-start | bytes 552968 | tf_op jit(solution)/shard_map/ppermute | solution.py:337
  60.1 1.8 %copy-start.27 = (bf16[1,3,180,3,64]{2,4,3,1,0:T(8,128)(2,1)S(1)}, bf16[1,3,180,3,64]{2,4,3,1,0:T(8,128)(2,1)}, u32[]{:S(2)}) copy-start(bf16[1,3,180,3,64]{2,4,3,1,0:T(8,128)(2,1)} %get-tuple-element.51) | copy-start | bytes 622084
  60.2 6.7 %collective-permute-start.7 = (bf16[32,8,180]{2,1,0:T(8,128)(2,1)S(1)}, bf16[32,8,180]{2,1,0:T(8,128)(2,1)S(1)}, u32[]{:S(2)}, u32[]{:S(2)}) collective-permute-start(bf16[32,8,180]{2,1,0:T(8,128)(2,1)S(1)} %get-tuple-element.79), channel_id=1, source_target_pairs={{0,7},{1,2},{2,1},{3,4},{4,3},{5,6},{6,5},{7,0},{8,15},{9,10},{10,... | collective-permute-start | bytes 276488 | tf_op jit(solution)/shard_map/ppermute | solution.py:337
  61.5 5.4 %collective-permute-start.6 = (bf16[32,8,180]{2,1,0:T(8,128)(2,1)S(1)}, bf16[32,8,180]{2,1,0:T(8,128)(2,1)S(1)}, u32[]{:S(2)}, u32[]{:S(2)}) collective-permute-start(bf16[32,8,180]{2,1,0:T(8,128)(2,1)S(1)} %get-tuple-element.80), channel_id=1, source_target_pairs={{0,1},{1,0},{2,3},{3,2},{4,5},{5,4},{6,7},{7,6},{8,9},{9,8},{10,11... | collective-permute-start | bytes 276488 | tf_op jit(solution)/shard_map/ppermute | solution.py:337
  66.9 7.6 %copy-start.32 = (bf16[1,180,360]{2,0,1:T(2,128)(2,1)S(1)}, bf16[1,180,360]{2,0,1:T(2,128)(2,1)}, u32[]{:S(2)}) copy-start(bf16[1,180,360]{2,0,1:T(2,128)(2,1)} %get-tuple-element.62) | copy-start | bytes 388804
  70.6 1.0 copy-start.8
  71.6 3.6 %copy-start.33 = (bf16[1,360,180]{1,0,2:T(2,128)(2,1)S(1)}, bf16[1,360,180]{1,0,2:T(2,128)(2,1)}, u32[]{:S(2)}) copy-start(bf16[1,360,180]{1,0,2:T(2,128)(2,1)} %get-tuple-element.58) | copy-start | bytes 388804
  71.6 25.6 %all-to-all-start.1 = ((f32[32,1,180]{2,1,0:T(1,128)}), f32[32,1,180]{2,1,0:T(1,128)S(1)}, u32[]{:S(2)}, u32[]{:S(2)}) async-start(f32[32,1,180]{2,1,0:T(1,128)} %get-tuple-element.36), calls=%async_computation.1 | async-start | bytes 65536 | tf_op jit(solution)/shard_map/all_to_all | solution.py:414
  97.9 1.2 copy-start.5
  99.1 1.2 copy-start.9
  105.7 9.5 %copy-start.26 = (bf16[1,3,180,3,64]{2,4,3,1,0:T(8,128)(2,1)S(1)}, bf16[1,3,180,3,64]{2,4,3,1,0:T(8,128)(2,1)}, u32[]{:S(2)}) copy-start(bf16[1,3,180,3,64]{2,4,3,1,0:T(8,128)(2,1)} %get-tuple-element.50) | copy-start | bytes 622084
  105.8 4.3 %collective-permute-start.8 = (bf16[2,64,180]{2,1,0:T(8,128)(2,1)S(1)}, bf16[2,64,180]{2,1,0:T(8,128)(2,1)S(1)}, u32[]{:S(2)}, u32[]{:S(2)}) collective-permute-start(bf16[2,64,180]{2,1,0:T(8,128)(2,1)S(1)} %get-tuple-element.39), channel_id=1, source_target_pairs={{0,8},{8,0},{16,24},{24,16},{1,9},{9,1},{17,25},{25,17},{2,10},{10... | collective-permute-start | bytes 138248 | tf_op jit(solution)/shard_map/ppermute | solution.py:337
  107.3 6.1 %collective-permute-start.9 = (bf16[2,64,180]{2,1,0:T(8,128)(2,1)S(1)}, bf16[2,64,180]{2,1,0:T(8,128)(2,1)S(1)}, u32[]{:S(2)}, u32[]{:S(2)}) collective-permute-start(bf16[2,64,180]{2,1,0:T(8,128)(2,1)S(1)} %get-tuple-element.40), channel_id=1, source_target_pairs={{0,24},{8,16},{16,8},{24,0},{1,25},{9,17},{17,9},{25,1},{2,26},{10... | collective-permute-start | bytes 138248 | tf_op jit(solution)/shard_map/ppermute | solution.py:337
  113.6 4.3 %collective-permute-start.11 = (bf16[20,2,180]{2,1,0:T(2,128)(2,1)S(1)}, bf16[20,2,180]{2,1,0:T(2,128)(2,1)S(1)}, u32[]{:S(2)}, u32[]{:S(2)}) collective-permute-start(bf16[20,2,180]{2,1,0:T(2,128)(2,1)S(1)} %get-tuple-element.103), channel_id=1, source_target_pairs={{0,7},{1,2},{2,1},{3,4},{4,3},{5,6},{6,5},{7,0},{8,15},{9,10},{10,... | collective-permute-start | bytes 43208 | tf_op jit(solution)/shard_map/ppermute | solution.py:337
  114.8 3.1 %collective-permute-start.10 = (bf16[20,2,180]{2,1,0:T(2,128)(2,1)S(1)}, bf16[20,2,180]{2,1,0:T(2,128)(2,1)S(1)}, u32[]{:S(2)}, u32[]{:S(2)}) collective-permute-start(bf16[20,2,180]{2,1,0:T(2,128)(2,1)S(1)} %get-tuple-element.104), channel_id=1, source_target_pairs={{0,1},{1,0},{2,3},{3,2},{4,5},{5,4},{6,7},{7,6},{8,9},{9,8},{10,11... | collective-permute-start | bytes 43208 | tf_op jit(solution)/shard_map/ppermute | solution.py:337
  117.9 8.2 %copy-start.30 = (bf16[1,180,360]{2,0,1:T(2,128)(2,1)S(1)}, bf16[1,180,360]{2,0,1:T(2,128)(2,1)}, u32[]{:S(2)}) copy-start(bf16[1,180,360]{2,0,1:T(2,128)(2,1)} %get-tuple-element.61) | copy-start | bytes 388804
  121.6 1.0 copy-start.6
  122.6 4.2 %copy-start.31 = (bf16[1,360,180]{1,0,2:T(2,128)(2,1)S(1)}, bf16[1,360,180]{1,0,2:T(2,128)(2,1)}, u32[]{:S(2)}) copy-start(bf16[1,360,180]{1,0,2:T(2,128)(2,1)} %get-tuple-element.57) | copy-start | bytes 388804
  122.6 13.7 %all-to-all-start.2 = ((f32[32,1,180]{2,1,0:T(1,128)}), f32[32,1,180]{2,1,0:T(1,128)S(1)}, u32[]{:S(2)}, u32[]{:S(2)}) async-start(f32[32,1,180]{2,1,0:T(1,128)} %get-tuple-element.42), calls=%async_computation.2 | async-start | bytes 65536 | tf_op jit(solution)/shard_map/all_to_all | solution.py:414
  126.8 1.0 copy-start.16
  136.3 1.2 copy-start.7
  142.3 10.7 %copy-start.11 = (bf16[16,64,180]{2,1,0:T(8,128)(2,1)}, bf16[16,64,180]{2,1,0:T(8,128)(2,1)S(1)}, u32[]{:S(2)}) copy-start(bf16[16,64,180]{2,1,0:T(8,128)(2,1)S(1)} %get-tuple-element.44.u_ref) | copy-start | bytes 1105924
  142.3 5.7 %collective-permute-start.12 = (bf16[4,64,180]{2,1,0:T(8,128)(2,1)S(1)}, bf16[4,64,180]{2,1,0:T(8,128)(2,1)S(1)}, u32[]{:S(2)}, u32[]{:S(2)}) collective-permute-start(bf16[4,64,180]{2,1,0:T(8,128)(2,1)S(1)} %get-tuple-element.45), channel_id=1, source_target_pairs={{0,8},{8,0},{16,24},{24,16},{1,9},{9,1},{17,25},{25,17},{2,10},{10... | collective-permute-start | bytes 276488 | tf_op jit(solution)/shard_map/ppermute | solution.py:337
  144.1 8.7 %collective-permute-start.13 = (bf16[4,64,180]{2,1,0:T(8,128)(2,1)S(1)}, bf16[4,64,180]{2,1,0:T(8,128)(2,1)S(1)}, u32[]{:S(2)}, u32[]{:S(2)}) collective-permute-start(bf16[4,64,180]{2,1,0:T(8,128)(2,1)S(1)} %get-tuple-element.46), channel_id=1, source_target_pairs={{0,24},{8,16},{16,8},{24,0},{1,25},{9,17},{17,9},{25,1},{2,26},{10... | collective-permute-start | bytes 276488 | tf_op jit(solution)/shard_map/ppermute | solution.py:337
  152.9 1.8 %copy-start.28 = (bf16[1,180,360]{2,0,1:T(2,128)(2,1)S(1)}, bf16[1,180,360]{2,0,1:T(2,128)(2,1)}, u32[]{:S(2)}) copy-start(bf16[1,180,360]{2,0,1:T(2,128)(2,1)} %get-tuple-element.60) | copy-start | bytes 388804
  152.9 1.8 %copy-start.29 = (bf16[1,360,180]{1,0,2:T(2,128)(2,1)S(1)}, bf16[1,360,180]{1,0,2:T(2,128)(2,1)}, u32[]{:S(2)}) copy-start(bf16[1,360,180]{1,0,2:T(2,128)(2,1)} %get-tuple-element.56) | copy-start | bytes 388804
  153.0 6.0 %copy-start.12 = (bf16[16,64,180]{2,1,0:T(8,128)(2,1)S(1)}, bf16[16,64,180]{2,1,0:T(8,128)(2,1)}, u32[]{:S(2)}) copy-start(bf16[16,64,180]{2,1,0:T(8,128)(2,1)} %copy-done.11) | copy-start | bytes 1105924
  153.0 6.0 %collective-permute-start.15 = (bf16[24,8,180]{2,1,0:T(8,128)(2,1)S(1)}, bf16[24,8,180]{2,1,0:T(8,128)(2,1)S(1)}, u32[]{:S(2)}, u32[]{:S(2)}) collective-permute-start(bf16[24,8,180]{2,1,0:T(8,128)(2,1)S(1)} %get-tuple-element.85), channel_id=1, source_target_pairs={{0,7},{1,2},{2,1},{3,4},{4,3},{5,6},{6,5},{7,0},{8,15},{9,10},{10,... | collective-permute-start | bytes 207368 | tf_op jit(solution)/shard_map/ppermute | solution.py:337
  154.3 4.7 %collective-permute-start.14 = (bf16[24,8,180]{2,1,0:T(8,128)(2,1)S(1)}, bf16[24,8,180]{2,1,0:T(8,128)(2,1)S(1)}, u32[]{:S(2)}, u32[]{:S(2)}) collective-permute-start(bf16[24,8,180]{2,1,0:T(8,128)(2,1)S(1)} %get-tuple-element.86), channel_id=1, source_target_pairs={{0,1},{1,0},{2,3},{3,2},{4,5},{5,4},{6,7},{7,6},{8,9},{9,8},{10,11... | collective-permute-start | bytes 207368 | tf_op jit(solution)/shard_map/ppermute | solution.py:337
  154.7 4.3 %copy-start.19 = (bf16[180,540]{1,0:T(8,128)(2,1)S(1)}, bf16[180,540]{1,0:T(8,128)(2,1)}, u32[]{:S(2)}) copy-start(bf16[180,540]{1,0:T(8,128)(2,1)} %qkv_ref.1) | copy-start | bytes 583204
  154.7 4.3 %copy-start.20 = (bf16[180,180]{1,0:T(8,128)(2,1)S(1)}, bf16[180,180]{1,0:T(8,128)(2,1)}, u32[]{:S(2)}) copy-start(bf16[180,180]{1,0:T(8,128)(2,1)} %proj_ref.1) | copy-start | bytes 194404
  (9 other events, 7.6 us)
where the time goes:
time: 176 us; the launch traced here: 175 us
  Pallas kernels  77.6 us (44%)
  waiting for transfers between devices  34.5 us (20%)
  starting transfers between devices  33.6 us (19%)
  local copies, waits for them, and re-layouts  29 us (16%)
    pallas_call x12, Pallas kernels, call(): pl.pallas_call(kernel, out_shape=outs, in_specs=specs, out_specs=jax.tree...  77.6 us
    ppermute x16, waiting for transfers between devices, swap(): return lax.ppermute(value, axis, pairs)  34.5 us
    ppermute x16, starting transfers between devices, swap(): return lax.ppermute(value, axis, pairs)  24.6 us
    unnamed x84, local copies, waits for them, and re-layouts  19.3 us
    all_to_all x3, starting transfers between devices, local(): sums = lax.all_to_all(sums, ('row', 'col'), 0, 0)  8.99 us
  transfers between devices with their start and end apart: 19, of which 10 were waited for; matrix products, arithmetic and copies ran while one was open for 7% of the time, Pallas kernels for 22%

commit v1 on v0

v1 whole, which is shorter than its diff:
```python
import functools
import math

import jax
import jax.numpy as jnp
from jax import lax
from jax.experimental import pallas as pl
from jax.experimental.pallas import tpu as pltpu
from jax.sharding import PartitionSpec as P

C = 180
HEADS = 6
HEAD = 30
WIN = 16
HID = 360
CC = 60
CP = 64
SHIFT = 8
OVL = 4
EDGE = 8
EPSILON = 1e-05
MASKED = -1000000000.0
BF16 = jnp.bfloat16
F32 = jnp.float32


def dot(a, b):
    return jnp.dot(a, b, preferred_element_type=F32)


def dot_nt(a, b):
    return lax.dot_general(a, b, (((1,), (1,)), ((), ())), preferred_element_type=F32)


def layer_norm(x):
    middle = jnp.sum(x, axis=-1, keepdims=True) * (1.0 / C)
    centered = x - middle
    spread = jnp.sum(centered * centered, axis=-1, keepdims=True) * (1.0 / C)
    return (centered * lax.rsqrt(spread + EPSILON)).astype(BF16)


def gelu(v):
    return v * (lax.erf(v * (0.5**0.5)) + 1.0) * 0.5


LANES = 256
SCALE = HEAD ** (-0.5) * math.log2(math.e)


def head_masks(rows, lanes):
    lane = lax.broadcasted_iota(jnp.int32, (rows, lanes), 1)
    return [(lane >= HEAD * h) & (lane < HEAD * (h + 1)) for h in range(HEADS)]


def attend(q, k, v, bias):
    n = q.shape[0]
    zero = jnp.zeros_like(q)
    stack = jnp.concatenate([jnp.where(mask, q, zero) for mask in head_masks(n, C)], axis=0)
    scores = dot_nt(stack, k)
    if bias is not None:
        scores = scores + bias
    highest = jnp.max(scores, axis=-1, keepdims=True)
    powers = jnp.exp2((scores - highest) * SCALE).astype(BF16)
    mixed = dot(powers, v)
    share = 1.0 / mixed[:, C : C + 1]
    mixed = mixed[:, :C] * share
    out = mixed[:n]
    for h, mask in enumerate(head_masks(n, C)):
        if h:
            out = jnp.where(mask, mixed[h * n : (h + 1) * n], out)
    return out.astype(BF16)


def split_qkv(w):
    wv = jnp.concatenate([w[:, 2 * C :], jnp.zeros((C, LANES - C), w.dtype)], axis=1)
    return w[:, :C], w[:, C : 2 * C], wv


def with_ones(v):
    lane = lax.broadcasted_iota(jnp.int32, v.shape, 1)
    return jnp.where(lane >= C, 1.0, v)


def norm_kernel(x_ref, u_ref):
    u_ref[...] = layer_norm(x_ref[...].astype(F32))


def window_kernel(k_at, start, count, u_ref, qkv_ref, proj_ref, after_ref, out_ref):
    wq, wk, wv = split_qkv(qkv_ref[k_at])
    proj = proj_ref[k_at]
    for i in range(u_ref.shape[0] // WIN):

        def body(j, carry):
            cols = pl.ds(pl.multiple_of((j + start) * WIN, WIN), WIN)
            rows = pl.ds(i * WIN, WIN)
            u = u_ref[rows, cols, :].reshape(WIN * WIN, C)
            q = dot(u, wq).astype(BF16)
            k = dot(u, wk).astype(BF16)
            v = with_ones(dot(u, wv)).astype(BF16)
            heads = attend(q, k, v, None)
            out_ref[rows, pl.ds(pl.multiple_of(j * WIN, WIN), WIN), :] = dot(
                heads, proj
            ).reshape(WIN, WIN, C)
            return carry

        lax.fori_loop(0, count, body, 0)


def place(ext, flags_ref, u_ref, row_e, row_o, col_e, col_o, width, left, convert):
    height, breadth = u_ref.shape[0], u_ref.shape[1]
    row_odd = flags_ref[0] == 1
    col_odd = flags_ref[1] == 1
    inside = [flags_ref[2 + s] == 1 for s in range(4)]

    def pick(cond, a, b, keep):
        value = jnp.where(cond, a[...].astype(F32), b[...].astype(F32))
        return convert(jnp.where(keep, value, 0.0))

    ext[width : width + height, left : left + breadth, :] = u_ref[...].astype(F32)
    ext[0:width, left : left + breadth, :] = pick(row_odd, row_e, row_o, inside[0])
    ext[width + height :, left : left + breadth, :] = pick(row_odd, row_o, row_e, inside[1])
    tall = height + 2 * width
    west = pick(col_odd, col_e, col_o, inside[2])
    east = pick(col_odd, col_o, col_e, inside[3])
    rows_at = lax.broadcasted_iota(jnp.int32, (tall, 1, 1), 0)
    real = ((rows_at >= width) | inside[0]) & ((rows_at < width + height) | inside[1])
    west = jnp.where(real, west.astype(F32), 0.0).astype(west.dtype)
    east = jnp.where(real, east.astype(F32), 0.0).astype(east.dtype)
    side = col_e.shape[1]
    ext[0:tall, left - side : left, :] = west
    ext[0:tall, left + breadth : left + breadth + side, :] = east


def shifted_kernel(
    k_at, i, flags_ref, u_ref, row_e, row_o, col_e, col_o, qkv_ref, proj_ref, after_ref, out_ref,
    ext, wide,
):
    height, breadth = u_ref.shape[0], u_ref.shape[1]
    place(ext, flags_ref, u_ref, row_e, row_o, col_e, col_o, SHIFT, SHIFT, lambda x: x)
    wq, wk, wv = split_qkv(qkv_ref[k_at])
    proj = proj_ref[k_at]
    north, south, west, east = [flags_ref[2 + s] == 1 for s in range(4)]
    count_i = height // WIN + 1
    count_j = breadth // WIN + 1
    key = lax.broadcasted_iota(jnp.int32, (1, WIN * WIN), 1)
    key_row, key_col = key // WIN, key % WIN
    low = SHIFT if i == 0 else 0
    high = SHIFT if i == count_i - 1 else WIN

    def body(j, carry):
        cols = pl.ds(pl.multiple_of(j * WIN, WIN), WIN)
        u = ext[i * WIN : (i + 1) * WIN, cols, :]
        part = u[low:high].reshape((high - low) * WIN, C).astype(BF16)
        u = u.reshape(WIN * WIN, C).astype(BF16)
        bad = jnp.zeros((1, WIN * WIN), jnp.bool_)
        if i == 0:
            bad = bad | ((key_row < SHIFT) & jnp.logical_not(north))
        if i == count_i - 1:
            bad = bad | ((key_row >= SHIFT) & jnp.logical_not(south))
        bad = bad | ((key_col < SHIFT) & (jnp.logical_not(west) & (j == 0)))
        bad = bad | ((key_col >= SHIFT) & (jnp.logical_not(east) & (j == count_j - 1)))
        bias = jnp.where(bad, MASKED, 0.0)
        q = dot(part, wq).astype(BF16)
        k = dot(u, wk).astype(BF16)
        v = with_ones(dot(u, wv)).astype(BF16)
        heads = attend(q, k, v, bias)
        wide[:, cols, :] = dot(heads, proj).reshape(high - low, WIN, C)
        return carry

    lax.fori_loop(0, count_j, body, 0)
    out_ref[...] = wide[:, SHIFT : SHIFT + breadth, :]


def cross_kernel(
    k_at, flags_ref, u_ref, row_e, row_o, col_e, col_o, qkv_ref, proj_ref, out_ref, ext, keys, values
):
    height, breadth = u_ref.shape[0], u_ref.shape[1]
    place(ext, flags_ref, u_ref, row_e, row_o, col_e, col_o, OVL, EDGE, lambda x: x)
    wq, wk, wv = split_qkv(qkv_ref[k_at] if len(qkv_ref.shape) == 3 else qkv_ref[...])
    proj = proj_ref[k_at] if len(proj_ref.shape) == 3 else proj_ref[...]
    tall, long = ext.shape[0], ext.shape[1]
    side = WIN + 2 * OVL
    flat = pltpu.roll(ext[...].reshape(tall * long, C), tall * long - (EDGE - OVL), 0)
    flat = flat.astype(BF16)
    keys[...] = dot(flat, wk).astype(BF16).astype(F32).reshape(tall, long, C)
    values[...] = with_ones(dot(flat, wv)).astype(BF16).astype(F32).reshape(tall, long, LANES)
    for i in range(height // WIN):

        def body(j, carry):
            at = j * WIN
            rows = pl.ds(i * WIN, WIN)
            u = u_ref[rows, pl.ds(at, WIN), :].reshape(WIN * WIN, C)
            q = dot(u, wq).astype(BF16)
            area = (pl.ds(i * WIN, side), pl.ds(at, side), slice(None))
            k = keys[area].reshape(side * side, C).astype(BF16)
            v = values[area].reshape(side * side, LANES).astype(BF16)
            heads = attend(q, k, v, None)
            out_ref[rows, pl.ds(at, WIN), :] = dot(heads, proj).reshape(WIN, WIN, C)
            return carry

        for j in range(breadth // WIN):
            body(j, 0)


def three_taps(ref, k_at, taps):
    pad = jnp.zeros((CP - CC, C), BF16)
    parts = []
    for t in taps:
        parts += [ref[k_at, t], pad]
    return jnp.concatenate(parts, axis=0)


def squeeze_kernel(
    k_at, width, raw, flags_ref, u_ref, row_e, row_o, col_e, col_o, w1_ref, w2_ref, after_ref,
    three_ref, sum_ref, ext,
):
    height, breadth = u_ref.shape[0], u_ref.shape[1]
    pitch = breadth + 2 * EDGE
    convert = (lambda x: layer_norm(x).astype(F32)) if raw else (lambda x: x)
    place(ext, flags_ref, u_ref, row_e, row_o, col_e, col_o, width, EDGE, convert)
    north, south, west, east = [flags_ref[2 + s] == 1 for s in range(4)]
    tall = height + 4
    first = width - 2
    flat = ext[first : first + tall].reshape(tall * pitch, C)
    acc = None
    for b in range(3):
        moved = flat if b == 1 else pltpu.roll(flat, (1 - b) % (tall * pitch), 0)
        part = dot_nt(moved.astype(BF16), three_taps(w1_ref, k_at, (b, 3 + b, 6 + b)))
        acc = part if acc is None else acc + part
    acc = acc.reshape(tall, pitch, 3 * CP)
    rows = height + 2
    pre = (
        acc[0:rows, :, 0:CP]
        + acc[1 : rows + 1, :, CP : 2 * CP]
        + acc[2 : rows + 2, :, 2 * CP : 3 * CP]
    )
    hidden = gelu(pre)
    row_at = lax.broadcasted_iota(jnp.int32, (rows, pitch, CP), 0)
    col_at = lax.broadcasted_iota(jnp.int32, (rows, pitch, CP), 1)
    real = ((row_at >= 1) | north) & ((row_at < rows - 1) | south)
    real = real & (col_at >= jnp.where(west, EDGE - 1, EDGE))
    real = real & (col_at < EDGE + breadth + jnp.where(east, 1, 0))
    hidden = jnp.where(real, hidden, 0.0).astype(BF16).astype(F32).reshape(rows * pitch, CP)
    total = rows * pitch
    three = jnp.concatenate(
        [pltpu.roll(hidden, 1, 0), hidden, pltpu.roll(hidden, total - 1, 0)], axis=1
    )
    three_ref[...] = three.astype(BF16)
    lines = jnp.sum(three.reshape(rows, pitch, 3 * CP)[:, EDGE : EDGE + breadth, :], axis=1)
    sums = jnp.zeros((1, C), F32)
    for a in range(3):
        box = jnp.sum(lines[a : a + height], axis=0, keepdims=True)
        high = box.astype(BF16)
        rest = box - high.astype(F32)
        middle = rest.astype(BF16)
        low = (rest - middle.astype(F32)).astype(BF16)
        taps = three_taps(w2_ref, k_at, (3 * a, 3 * a + 1, 3 * a + 2))
        for piece in (high, middle, low):
            wide = jnp.broadcast_to(piece.astype(F32), (16, 3 * CP)).astype(BF16)
            sums = sums + dot(wide, taps)[0:1]
    sum_ref[...] = sums


def expand_kernel(k_at, three_ref, w2_ref, after_ref, out_ref):
    height, breadth = out_ref.shape[0], out_ref.shape[1]
    pitch = breadth + 2 * EDGE
    out = None
    for a in range(3):
        part = dot(
            three_ref[a * pitch : (a + height) * pitch, :],
            three_taps(w2_ref, k_at, (3 * a, 3 * a + 1, 3 * a + 2)),
        )
        out = part if out is None else out + part
    out_ref[...] = out.reshape(height, pitch, C)[:, EDGE : EDGE + breadth, :]


def ff_tail(k_at, x, in_ref, out_w_ref):
    hidden = gelu(dot(layer_norm(x), in_ref[k_at])).astype(BF16)
    return x + dot(hidden, out_w_ref[k_at])


def block_kernel(
    k_at, rim, area, pieces, by_rows, flags_ref, x_ref, exp_ref, sums_ref, down_ref, up_ref, in_ref,
    out_w_ref, *refs,
):
    att_refs = refs[:pieces]
    y_ref, u_ref = refs[pieces : pieces + 2]
    rim_refs = refs[pieces + 2 :]
    pooled = sums_ref[...] * (1.0 / area)
    squeezed = jnp.sum(down_ref[k_at].astype(F32) * pooled, axis=-1, keepdims=True)
    squeezed = jnp.maximum(squeezed, 0.0)
    gate = jax.nn.sigmoid(jnp.sum(up_ref[k_at].astype(F32) * squeezed, axis=0, keepdims=True))
    height, breadth = x_ref.shape[0], x_ref.shape[1]
    step = 4

    def chunk(rows, att):
        x = x_ref[rows].reshape(step * breadth, C).astype(F32)
        x = x + att.reshape(step * breadth, C)
        x = x + exp_ref[rows].reshape(step * breadth, C) * gate
        y = ff_tail(k_at, x, in_ref, out_w_ref)
        y_ref[rows] = y.reshape(step, breadth, C)
        u_ref[rows] = layer_norm(y).reshape(step, breadth, C)

    if by_rows:
        part = height // pieces
        for p in range(pieces):

            def body(r, carry):
                chunk(pl.ds(p * part + r * step, step), att_refs[p][pl.ds(r * step, step)])
                return carry

            lax.fori_loop(0, part // step, body, 0)
    else:

        def body(r, carry):
            rows = pl.ds(r * step, step)
            chunk(rows, jnp.concatenate([ref[rows] for ref in att_refs], axis=1))
            return carry

        lax.fori_loop(0, height // step, body, 0)
    for index, width in enumerate(rim):
        rims(width, flags_ref, u_ref, rim_refs[2 * index], rim_refs[2 * index + 1])


def rims(rim, flags_ref, u_ref, even_ref, odd_ref):
    height = u_ref.shape[0]
    head = u_ref[0:rim]
    tail = u_ref[height - rim :]
    odd = flags_ref[0] == 1

    @pl.when(odd)
    def _():
        even_ref[...] = head
        odd_ref[...] = tail

    @pl.when(jnp.logical_not(odd))
    def _():
        even_ref[...] = tail
        odd_ref[...] = head


def first_kernel(x_ref, u_ref):
    u_ref[...] = layer_norm(x_ref[...].astype(F32))


def last_kernel(k_at, x_ref, att_ref, in_ref, out_w_ref, y_ref):
    height, breadth = x_ref.shape[0], x_ref.shape[1]
    step = 4

    def body(r, carry):
        rows = pl.ds(r * step, step)
        x = (x_ref[rows] + att_ref[rows]).reshape(step * breadth, C)
        y = ff_tail(k_at, x, in_ref, out_w_ref)
        y_ref[rows] = y.astype(BF16).reshape(step, breadth, C)
        return carry

    lax.fori_loop(0, height // step, body, 0)


VM = pl.BlockSpec(memory_space=pltpu.VMEM)
SM = pl.BlockSpec(memory_space=pltpu.SMEM)
ANY = pl.BlockSpec(memory_space=pl.ANY)


def call(kernel, name, outs, scratch, flags, *args, after=None, limit=20):
    specs = [VM] * len(args)
    if flags is not None:
        specs = [SM] + specs
        args = (flags,) + args
    if after is not None:
        specs = specs + [ANY]
        args = args + (after,)
    return pl.pallas_call(
        kernel,
        out_shape=outs,
        in_specs=specs,
        out_specs=jax.tree.map(lambda _: VM, outs),
        scratch_shapes=scratch,
        name=name,
        compiler_params=pltpu.CompilerParams(vmem_limit_bytes=limit * 1024 * 1024),
    )(*args)


def swap(value, axis, odd, ring=True):
    count = lax.axis_size(axis)
    pairs = []
    for i in range(count):
        other = i + (1 if (i % 2 == 0) != odd else -1)
        if ring or 0 <= other < count:
            pairs.append((i, other % count))
    return lax.ppermute(value, axis, pairs)


def groups_of(count, first):
    bits = [1 << b for b in range(count.bit_length() - 1)]
    groups = [[b] for b in bits[:first]]
    rest = bits[first:]
    return groups + [rest[i : i + 2] for i in range(0, len(rest), 2)]


def all_sum_steps():
    steps = []
    for axis, first in (("col", 1), ("row", 0)):
        count = lax.axis_size(axis)
        for group in groups_of(count, first):
            masks = [group[0]] if len(group) == 1 else [group[0], group[1], group[0] + group[1]]
            steps.append((axis, count, masks))
    return steps


def sum_step(value, step):
    axis, count, masks = step
    got = [lax.ppermute(value, axis, [(i, i ^ m) for i in range(count)]) for m in masks]
    return functools.reduce(jnp.add, got, value)


def exchange_rows(even, odd, ring):
    return swap(even, "row", False), swap(odd, "row", True, ring)


def exchange_cols(u, row_e, row_o, side, flags):
    row_odd = flags[0] == 1
    col_odd = flags[1] == 1
    above = jnp.where(row_odd, row_e, row_o)
    below = jnp.where(row_odd, row_o, row_e)
    breadth = u.shape[1]
    head = jnp.concatenate([a[:, :side] for a in (above, u, below)], axis=0)
    tail = jnp.concatenate([a[:, breadth - side :] for a in (above, u, below)], axis=0)
    col_e = swap(jnp.where(col_odd, head, tail), "col", False)
    col_o = swap(jnp.where(col_odd, tail, head), "col", True)
    return col_e, col_o


def local(
    scene_tokens, block_qkv, block_proj, conv_squeeze, conv_expand, gate_down, gate_up,
    mlp_in, mlp_out, ocab_qkv, ocab_proj,
):
    height, breadth = scene_tokens.shape[0], scene_tokens.shape[1]
    row_count, col_count = lax.axis_size("row"), lax.axis_size("col")
    area = height * row_count * breadth * col_count
    row, col = lax.axis_index("row"), lax.axis_index("col")
    flags = jnp.stack(
        [
            row % 2,
            col % 2,
            (row > 0).astype(jnp.int32),
            (row < row_count - 1).astype(jnp.int32),
            (col > 0).astype(jnp.int32),
            (col < col_count - 1).astype(jnp.int32),
        ]
    ).astype(jnp.int32)
    w1 = conv_squeeze.swapaxes(2, 3)
    down = gate_down.swapaxes(1, 2)

    def shape(rows, cols, dtype):
        return jax.ShapeDtypeStruct((rows, cols, C), dtype)

    tile = shape(height, breadth, F32)
    tile16 = shape(height, breadth, BF16)
    pitch = breadth + 2 * EDGE
    hidden_shape = jax.ShapeDtypeStruct(((height + 2) * pitch, 3 * CP), BF16)
    narrow = 2
    windows = breadth // WIN
    half, quarter = windows // 2, windows // 4
    cuts = [(0, half), (half, quarter), (half + quarter, windows - half - quarter)]

    def rim_shapes(widths):
        return sum(((shape(w, breadth, BF16),) * 2 for w in widths), ())

    def window_piece(k, u, piece, after):
        start, count = cuts[piece]
        return call(
            functools.partial(window_kernel, k, start, count), "window_attention",
            shape(height, count * WIN, F32), [], None, u, block_qkv, block_proj, after=after,
        )

    def squeeze(k, u, rows, cols, after):
        return call(
            functools.partial(squeeze_kernel, k, narrow, k == 0), "squeeze",
            (hidden_shape, jax.ShapeDtypeStruct((1, C), F32)),
            [pltpu.VMEM((height + 2 * narrow, pitch, C), F32)],
            flags, u, *rows, *cols, w1, conv_expand, after=after,
        )

    def expand(k, three, after):
        return call(
            functools.partial(expand_kernel, k), "expand", tile, [], None, three, conv_expand,
            after=after,
        )

    row_odd = flags[0] == 1
    head, tail = scene_tokens[:narrow], scene_tokens[height - narrow :]
    even, odd = jnp.where(row_odd, head, tail), jnp.where(row_odd, tail, head)
    source = scene_tokens
    stream = scene_tokens
    u = call(first_kernel, "norm", tile16, [], None, scene_tokens)
    rim = [even, odd]
    steps = all_sum_steps()
    for k in range(3):
        rows = exchange_rows(rim[0], rim[1], True)
        if k == 1:
            rows8 = exchange_rows(rim[2], rim[3], False)
            cols = exchange_cols(u, *rows, narrow, flags)
            three, sums = squeeze(k, u, rows, cols, u)
            sums = sum_step(sums, steps[0])
            expanded = expand(k, three, sums)
            cols8 = exchange_cols(u, *rows8, SHIFT, flags)
            tall, long = height + 2 * SHIFT, breadth + 2 * SHIFT
            pieces = []
            for i in range(height // WIN + 1):
                if i < len(steps) - 1:
                    sums = sum_step(sums, steps[1 + i])
                pieces.append(
                    call(
                        functools.partial(shifted_kernel, k, i), "shifted_attention",
                        shape(WIN // 2, breadth, F32),
                        [pltpu.VMEM((tall, long, C), F32), pltpu.VMEM((WIN // 2, long, C), F32)],
                        flags, u, *rows8, *cols8, block_qkv, block_proj,
                        after=pieces[-1] if pieces else expanded,
                    )
                )
            for step in steps[1 + height // WIN + 1 :]:
                sums = sum_step(sums, step)
            by_rows = True
        else:
            first = window_piece(k, u, 0, u)
            cols = exchange_cols(source, *rows, narrow, flags)
            second = window_piece(k, u, 1, first)
            three, sums = squeeze(k, u, rows, cols, second)
            sums = sum_step(sums, steps[0])
            expanded = expand(k, three, sums)
            third = window_piece(k, u, 2, expanded)
            for step in steps[1:]:
                sums = sum_step(sums, step)
            pieces = [first, second, third]
            by_rows = False
        widths = {0: [narrow, SHIFT], 1: [narrow], 2: [OVL]}[k]
        stream, u, *rim = call(
            functools.partial(block_kernel, k, widths, area, len(pieces), by_rows), "feed_forward",
            (tile, tile16) + rim_shapes(widths), [],
            flags, stream, expanded, sums, down, gate_up, mlp_in, mlp_out, *pieces,
        )
        source = u
    rows = exchange_rows(*rim, True)
    cols = exchange_cols(u, *rows, EDGE, flags)
    tall, long = height + 2 * OVL, breadth + 2 * EDGE
    att = call(
        functools.partial(cross_kernel, 0), "cross_attention", tile,
        [pltpu.VMEM((tall, long, C), F32)] * 2 + [pltpu.VMEM((tall, long, LANES), F32)],
        flags, u, *rows, *cols, ocab_qkv, ocab_proj,
    )
    return call(
        functools.partial(last_kernel, 3), "last", tile16, [], None, stream, att, mlp_in, mlp_out
    )


def solution(mesh):
    return jax.shard_map(
        local,
        mesh=mesh,
        in_specs=(P("row", "col", None),) + (P(),) * 10,
        out_specs=P("row", "col", None),
        check_vma=False,
    )
```

time: 176 us -> 158 us (0.90)
  local copies, waits for them, and re-layouts: 29 us -> 8.8 us
  Pallas kernels: 77.6 us -> 61.3 us
  starting transfers between devices: 33.6 us -> 46.5 us
  waiting for transfers between devices: 34.5 us -> 38.8 us
    ppermute x0 -> x21, starting transfers between devices: none -> 24.5 us  [sum_step(): lax.ppermute(value, axis, [(i, i ^ m) for i in range(count)])]
    pallas_call x12 -> x20, Pallas kernels: 77.6 us -> 61.3 us  [call(): pl.pallas_call(kernel, out_shape=outs, in_specs=specs, out_specs=jax.tree...]
    ppermute x0 -> x21, waiting for transfers between devices: none -> 12.7 us  [sum_step(): lax.ppermute(value, axis, [(i, i ^ m) for i in range(count)])]
    unnamed x84 -> x40, local copies, waits for them, and re-layouts: 19.3 us -> 7.67 us
    all_to_all x3 -> x0, starting transfers between devices: 8.99 us -> none  [local(): sums = lax.all_to_all(sums, ('row', 'col'), 0, 0)]
    ppermute x16 -> x20, waiting for transfers between devices: 34.5 us -> 26 us  [swap(): return lax.ppermute(value, axis, pairs)]
    slice x15 -> x14, local copies, waits for them, and re-layouts: 5.8 us -> 1.05 us  [exchange_cols(): head = jnp.concatenate([a[:, :side] for a in (above, u, below)], axis=0)]
    squeeze x6 -> x0, local copies, waits for them, and re-layouts: 3.68 us -> none  [the longest x1 1.8 us: local(): block_proj[k]]
  transfers between devices with their start and end apart: 19 -> 41, of which waited for: 10 -> 23; matrix products, arithmetic and copies ran while one was open for 7% -> 2% of each run, Pallas kernels for 22% -> 11%
where the time goes in v1:
time: 158 us; the launch traced here: 157 us
  Pallas kernels  61.3 us (39%)
  starting transfers between devices  46.5 us (29%)
  waiting for transfers between devices  38.8 us (25%)
  local copies, waits for them, and re-layouts  8.8 us (6%)
    pallas_call x20, Pallas kernels, call(): pl.pallas_call(kernel, out_shape=outs, in_specs=specs, out_specs=jax.tree...  61.3 us
    ppermute x20, waiting for transfers between devices, swap(): return lax.ppermute(value, axis, pairs)  26 us
    ppermute x21, starting transfers between devices, sum_step(): lax.ppermute(value, axis, [(i, i ^ m) for i in range(count)])  24.5 us
    ppermute x20, starting transfers between devices, swap(): return lax.ppermute(value, axis, pairs)  22 us
    ppermute x21, waiting for transfers between devices, sum_step(): lax.ppermute(value, axis, [(i, i ^ m) for i in range(count)])  12.7 us
    unnamed x40, local copies, waits for them, and re-layouts  7.67 us
  transfers between devices with their start and end apart: 41, of which 23 were waited for; matrix products, arithmetic and copies ran while one was open for 2% of the time, Pallas kernels for 11%

profile of v1, /device:TPU:0, one launch (start us, length us, event | category | flops | bytes accessed | tf_op | source)
XLA Modules:
  0.0 157.5 jit_solution(7971665249870355068)
XLA Ops:
  0.9 5.1 %collective-permute-start.1 = (bf16[2,64,180]{2,1,0:T(8,128)(2,1)S(1)}, bf16[2,64,180]{2,1,0:T(8,128)(2,1)S(1)}, u32[]{:S(2)}, u32[]{:S(2)}) collective-permute-start(bf16[2,64,180]{2,1,0:T(8,128)(2,1)S(1)} %get-tuple-element.57), channel_id=1, source_target_pairs={{0,24},{8,16},{16,8},{24,0},{1,25},{9,17},{17,9},{25,1},{2,26},{10... | collective-permute-start | bytes 138248 | tf_op jit(solution)/shard_map/ppermute | solution.py:391
  7.0 2.0 %collective-permute-done.1.row_o = bf16[2,64,180]{2,1,0:T(8,128)(2,1)S(1)} collective-permute-done((bf16[2,64,180]{2,1,0:T(8,128)(2,1)S(1)}, bf16[2,64,180]{2,1,0:T(8,128)(2,1)S(1)}, u32[]{:S(2)}, u32[]{:S(2)}) %collective-permute-start.1) | collective-permute-done | bytes 46112 | tf_op jit(solution)/shard_map/ppermute | solution.py:391
  9.0 1.4 collective-permute-done.row_e
  13.1 3.7 %window_attention.6.after_ref.refs_0_ = f32[16,32,180]{2,1,0:T(8,128)S(1)} custom-call(bf16[16,64,180]{2,1,0:T(8,128)(2,1)S(1)} %norm.1.u_ref.after_ref, bf16[3,180,540]{2,1,0:T(8,128)(2,1)S(1)} %copy-done, bf16[3,180,180]{2,1,0:T(8,128)(2,1)S(1)} %copy-done.2, bf16[16,64,180]{2,1,0:T(8,128)(2,1)S(1)} %norm.1.u_ref.after_ref), custom_call_target="tpu_custom_call" | custom-call | tf_op jit(solution)/shard_map/window_attention/pallas_call | solution.py:373
  16.8 1.8 %window_attention.7.after_ref.refs_1_ = f32[16,16,180]{2,1,0:T(8,128)S(1)} custom-call(bf16[16,64,180]{2,1,0:T(8,128)(2,1)S(1)} %norm.1.u_ref.after_ref, bf16[3,180,540]{2,1,0:T(8,128)(2,1)S(1)} %copy-done, bf16[3,180,180]{2,1,0:T(8,128)(2,1)S(1)} %copy-done.2, f32[16,32,180]{2,1,0:T(8,128)S(1)} %window_attention.6.after_ref.refs_0_), custom_call_target="tpu_custom_call" | custom-call | tf_op jit(solution)/shard_map/window_attention/pallas_call | solution.py:373
  19.3 1.2 copy-done.4
  21.2 2.5 %squeeze.3 = (bf16[1440,192]{1,0:T(8,128)(2,1)S(1)}, f32[1,180]{1,0:T(1,128)S(1)}) custom-call(s32[6]{0:T(128)S(1)} %stack.43.flags_ref, bf16[16,64,180]{2,1,0:T(8,128)(2,1)S(1)} %norm.1.u_ref.after_ref, bf16[2,64,180]{2,1,0:T(8,128)(2,1)S(1)} %collective-permute-done.row_e, bf16[2,64,180]{2,1,0:T(8,128)(2,1)S(1)} %collective-permute-done.1.row_o, ...), custom_call_target="tpu_custom_call" | custom-call | tf_op jit(solution)/shard_map/squeeze/pallas_call | solution.py:373
  24.6 1.2 collective-permute-done.4
  25.8 1.4 collective-permute-start.7
  27.2 1.5 collective-permute-start.6
  30.8 1.5 collective-permute-done.5
  32.3 2.1 %collective-permute-start.10 = (f32[1,180]{1,0:T(1,128)S(1)}, f32[1,180]{1,0:T(1,128)S(1)}, u32[]{:S(2)}, u32[]{:S(2)}) collective-permute-start(f32[1,180]{1,0:T(1,128)S(1)} %add_add_fusion.5), channel_id=1, source_target_pairs={{0,24},{8,16},{16,8},{24,0},{1,25},{9,17},{17,9},{25,1},{2,26},{10... | collective-permute-start | bytes 2168 | tf_op jit(solution)/shard_map/ppermute | solution.py:413
  34.7 2.0 %collective-permute-start.8 = (f32[1,180]{1,0:T(1,128)S(1)}, f32[1,180]{1,0:T(1,128)S(1)}, u32[]{:S(2)}, u32[]{:S(2)}) collective-permute-start(f32[1,180]{1,0:T(1,128)S(1)} %add_add_fusion.5), channel_id=1, source_target_pairs={{0,8},{8,0},{16,24},{24,16},{1,9},{9,1},{17,25},{25,17},{2,10},{10... | collective-permute-start | bytes 2168 | tf_op jit(solution)/shard_map/ppermute | solution.py:413
  37.6 1.6 %copy.13.out_w_ref = bf16[4,360,180]{2,1,0:T(8,128)(2,1)S(1)} copy(bf16[4,360,180]{1,0,2:T(4,128)(2,1)} %param.19) | data formatting | bytes 1036800 | tf_op args[8]
  41.1 1.8 %window_attention.8.refs_2_ = f32[16,16,180]{2,1,0:T(8,128)S(1)} custom-call(bf16[16,64,180]{2,1,0:T(8,128)(2,1)S(1)} %norm.1.u_ref.after_ref, bf16[3,180,540]{2,1,0:T(8,128)(2,1)S(1)} %copy-done, bf16[3,180,180]{2,1,0:T(8,128)(2,1)S(1)} %copy-done.2, f32[16,64,180]{2,1,0:T(8,128)S(1)} %expand.3.after_ref.exp_ref), custom_call_target="tpu_custom_call" | custom-call | tf_op jit(solution)/shard_map/window_attention/pallas_call | solution.py:373
  43.0 3.6 %feed_forward.3 = (f32[16,64,180]{2,1,0:T(8,128)S(1)}, bf16[16,64,180]{2,1,0:T(8,128)(2,1)S(1)}, bf16[2,64,180]{2,1,0:T(8,128)(2,1)S(1)}, bf16[2,64,180]{2,1,0:T...) custom-call(s32[6]{0:T(128)S(1)} %stack.43.flags_ref, ...), custom_call_target="tpu_custom_call" | custom-call | tf_op jit(solution)/shard_map/feed_forward/pallas_call | solution.py:373
  46.7 2.1 %collective-permute-start.12 = (bf16[2,64,180]{2,1,0:T(8,128)(2,1)S(1)}, bf16[2,64,180]{2,1,0:T(8,128)(2,1)S(1)}, u32[]{:S(2)}, u32[]{:S(2)}) collective-permute-start(bf16[2,64,180]{2,1,0:T(8,128)(2,1)S(1)} %get-tuple-element.30), channel_id=1, source_target_pairs={{0,24},{8,16},{16,8},{24,0},{1,25},{9,17},{17,9},{25,1},{2,26},{10... | collective-permute-start | bytes 138248 | tf_op jit(solution)/shard_map/ppermute | solution.py:391
  48.8 2.1 %collective-permute-done.11.row_e = bf16[2,64,180]{2,1,0:T(8,128)(2,1)S(1)} collective-permute-done((bf16[2,64,180]{2,1,0:T(8,128)(2,1)S(1)}, bf16[2,64,180]{2,1,0:T(8,128)(2,1)S(1)}, u32[]{:S(2)}, u32[]{:S(2)}) %collective-permute-start.11) | collective-permute-done | bytes 46112 | tf_op jit(solution)/shard_map/ppermute | solution.py:391
  50.9 2.0 %collective-permute-done.12.row_o = bf16[2,64,180]{2,1,0:T(8,128)(2,1)S(1)} collective-permute-done((bf16[2,64,180]{2,1,0:T(8,128)(2,1)S(1)}, bf16[2,64,180]{2,1,0:T(8,128)(2,1)S(1)}, u32[]{:S(2)}, u32[]{:S(2)}) %collective-permute-start.12) | collective-permute-done | bytes 46112 | tf_op jit(solution)/shard_map/ppermute | solution.py:391
  53.7 3.5 %collective-permute-done.14.col_o = bf16[20,2,180]{2,1,0:T(2,128)(2,1)S(1)} collective-permute-done((bf16[20,2,180]{2,1,0:T(2,128)(2,1)S(1)}, bf16[20,2,180]{2,1,0:T(2,128)(2,1)S(1)}, u32[]{:S(2)}, u32[]{:S(2)}) %collective-permute-start.14) | collective-permute-done | bytes 14432 | tf_op jit(solution)/shard_map/ppermute | solution.py:391
  57.2 2.2 %squeeze.4 = (bf16[1440,192]{1,0:T(8,128)(2,1)S(1)}, f32[1,180]{1,0:T(1,128)S(1)}) custom-call(s32[6]{0:T(128)S(1)} %stack.43.flags_ref, bf16[16,64,180]{2,1,0:T(8,128)(2,1)S(1)} %get-tuple-element.28.u_ref.after_ref, bf16[2,64,180]{2,1,0:T(8,128)(2,1)S(1)} %collective-permute-done.11.row_e, bf16[2,64,180]{2,1,0:T(8,128)(2,1)S(1)} %collective-permute-done.12.row_o, ...), custom_call_target="tpu_custom_call" | custom-call | tf_op jit(solution)/shard_map/squeeze/pallas_call | solution.py:373
  59.4 1.2 collective-permute-done.15
  61.8 2.2 %collective-permute-start.16 = (f32[1,180]{1,0:T(1,128)S(1)}, f32[1,180]{1,0:T(1,128)S(1)}, u32[]{:S(2)}, u32[]{:S(2)}) collective-permute-start(f32[1,180]{1,0:T(1,128)S(1)} %add.79.after_ref), channel_id=1, source_target_pairs={{0,2},{1,3},{2,0},{3,1},{4,6},{5,7},{6,4},{7,5},{8,10},{9,11},{10,... | collective-permute-start | bytes 2168 | tf_op jit(solution)/shard_map/ppermute | solution.py:413
  66.4 2.1 %collective-permute-start.21 = (f32[1,180]{1,0:T(1,128)S(1)}, f32[1,180]{1,0:T(1,128)S(1)}, u32[]{:S(2)}, u32[]{:S(2)}) collective-permute-start(f32[1,180]{1,0:T(1,128)S(1)} %add_add_fusion.3), channel_id=1, source_target_pairs={{0,24},{8,16},{16,8},{24,0},{1,25},{9,17},{17,9},{25,1},{2,26},{10... | collective-permute-start | bytes 2168 | tf_op jit(solution)/shard_map/ppermute | solution.py:413
  68.6 3.1 %collective-permute-start.20 = (f32[1,180]{1,0:T(1,128)S(1)}, f32[1,180]{1,0:T(1,128)S(1)}, u32[]{:S(2)}, u32[]{:S(2)}) collective-permute-start(f32[1,180]{1,0:T(1,128)S(1)} %add_add_fusion.3), channel_id=1, source_target_pairs={{0,16},{8,24},{16,0},{24,8},{1,17},{9,25},{17,1},{25,9},{2,18},{10... | collective-permute-start | bytes 2168 | tf_op jit(solution)/shard_map/ppermute | solution.py:413
  72.6 2.2 %collective-permute-done.20 = f32[1,180]{1,0:T(1,128)S(1)} collective-permute-done((f32[1,180]{1,0:T(1,128)S(1)}, f32[1,180]{1,0:T(1,128)S(1)}, u32[]{:S(2)}, u32[]{:S(2)}) %collective-permute-start.20) | collective-permute-done | bytes 752 | tf_op jit(solution)/shard_map/ppermute | solution.py:413
  75.2 1.9 %collective-permute-done.25.col_o = bf16[32,8,180]{2,1,0:T(8,128)(2,1)S(1)} collective-permute-done((bf16[32,8,180]{2,1,0:T(8,128)(2,1)S(1)}, bf16[32,8,180]{2,1,0:T(8,128)(2,1)S(1)}, u32[]{:S(2)}, u32[]{:S(2)}) %collective-permute-start.25) | collective-permute-done | bytes 92192 | tf_op jit(solution)/shard_map/ppermute | solution.py:391
  77.2 6.2 %shifted_attention.2.after_ref.refs_0_ = f32[8,64,180]{2,1,0:T(8,128)S(1)} custom-call(s32[6]{0:T(128)S(1)} %stack.43.flags_ref, bf16[16,64,180]{2,1,0:T(8,128)(2,1)S(1)} %get-tuple-element.28.u_ref.after_ref, bf16[8,64,180]{2,1,0:T(8,128)(2,1)S(1)} %collective-permute-done.22.row_e, bf16[8,64,180]{2,1,0:T(8,128)(2,1)S(1)} %collective-permute-done.23.row_o, ...), custom_call_target="tpu_custom_call" | custom-call | tf_op jit(solution)/shard_map/shifted_attention/pallas_call | solution.py:373
  83.4 6.2 %shifted_attention.3.refs_1_ = f32[8,64,180]{2,1,0:T(8,128)S(1)} custom-call(s32[6]{0:T(128)S(1)} %stack.43.flags_ref, bf16[16,64,180]{2,1,0:T(8,128)(2,1)S(1)} %get-tuple-element.28.u_ref.after_ref, bf16[8,64,180]{2,1,0:T(8,128)(2,1)S(1)} %collective-permute-done.22.row_e, bf16[8,64,180]{2,1,0:T(8,128)(2,1)S(1)} %collective-permute-done.23.row_o, ...), custom_call_target="tpu_custom_call" | custom-call | tf_op jit(solution)/shard_map/shifted_attention/pallas_call | solution.py:373
  89.6 3.5 %feed_forward.4 = (f32[16,64,180]{2,1,0:T(8,128)S(1)}, bf16[16,64,180]{2,1,0:T(8,128)(2,1)S(1)}, bf16[2,64,180]{2,1,0:T(8,128)(2,1)S(1)}, bf16[2,64,180]{2,1,0:T(8,128)(2,1)S(1)}) custom-call(s32[6]{0:T(128)S(1)} %stack.43.flags_ref, f32[16,64,180]{2,1,0:T(8,128)S(1)} %get-tuple-element.27.x_ref, f32[16,64,180]{2,1,0:T(8,128)S(1)} %expand.4.after_ref.exp_ref, ...), custom_call_target="tpu_custom_call" | custom-call | tf_op jit(solution)/shard_map/feed_forward/pallas_call | solution.py:373
  93.2 3.7 %collective-permute-start.26 = (bf16[2,64,180]{2,1,0:T(8,128)(2,1)S(1)}, bf16[2,64,180]{2,1,0:T(8,128)(2,1)S(1)}, u32[]{:S(2)}, u32[]{:S(2)}) collective-permute-start(bf16[2,64,180]{2,1,0:T(8,128)(2,1)S(1)} %get-tuple-element.37), channel_id=1, source_target_pairs={{0,8},{8,0},{16,24},{24,16},{1,9},{9,1},{17,25},{25,17},{2,10},{10... | collective-permute-start | bytes 138248 | tf_op jit(solution)/shard_map/ppermute | solution.py:391
  96.9 2.1 %collective-permute-start.27 = (bf16[2,64,180]{2,1,0:T(8,128)(2,1)S(1)}, bf16[2,64,180]{2,1,0:T(8,128)(2,1)S(1)}, u32[]{:S(2)}, u32[]{:S(2)}) collective-permute-start(bf16[2,64,180]{2,1,0:T(8,128)(2,1)S(1)} %get-tuple-element.38), channel_id=1, source_target_pairs={{0,24},{8,16},{16,8},{24,0},{1,25},{9,17},{17,9},{25,1},{2,26},{10... | collective-permute-start | bytes 138248 | tf_op jit(solution)/shard_map/ppermute | solution.py:391
  99.2 3.8 %collective-permute-done.27.row_o = bf16[2,64,180]{2,1,0:T(8,128)(2,1)S(1)} collective-permute-done((bf16[2,64,180]{2,1,0:T(8,128)(2,1)S(1)}, bf16[2,64,180]{2,1,0:T(8,128)(2,1)S(1)}, u32[]{:S(2)}, u32[]{:S(2)}) %collective-permute-start.27) | collective-permute-done | bytes 46112 | tf_op jit(solution)/shard_map/ppermute | solution.py:391
  103.8 3.7 %window_attention.9.after_ref.refs_0_ = f32[16,32,180]{2,1,0:T(8,128)S(1)} custom-call(bf16[16,64,180]{2,1,0:T(8,128)(2,1)S(1)} %get-tuple-element.36.u_ref.after_ref, bf16[3,180,540]{2,1,0:T(8,128)(2,1)S(1)} %copy-done, bf16[3,180,180]{2,1,0:T(8,128)(2,1)S(1)} %copy-done.2, bf16[16,64,180]{2,1,0:T(8,128)(2,1)S(1)} %get-tuple-element.36.u_ref.after_ref), custom_call_target="tpu_custom_call" | custom-call | tf_op jit(solution)/shard_map/window_attention/pallas_call | solution.py:373
  107.5 1.8 %window_attention.10.after_ref.refs_1_ = f32[16,16,180]{2,1,0:T(8,128)S(1)} custom-call(bf16[16,64,180]{2,1,0:T(8,128)(2,1)S(1)} %get-tuple-element.36.u_ref.after_ref, bf16[3,180,540]{2,1,0:T(8,128)(2,1)S(1)} %copy-done, bf16[3,180,180]{2,1,0:T(8,128)(2,1)S(1)} %copy-done.2, f32[16,32,180]{2,1,0:T(8,128)S(1)} %window_attention.9.after_ref.refs_0_), custom_call_target="tpu_custom_call" | custom-call | tf_op jit(solution)/shard_map/window_attention/pallas_call | solution.py:373
  109.3 2.2 %squeeze.5 = (bf16[1440,192]{1,0:T(8,128)(2,1)S(1)}, f32[1,180]{1,0:T(1,128)S(1)}) custom-call(s32[6]{0:T(128)S(1)} %stack.43.flags_ref, bf16[16,64,180]{2,1,0:T(8,128)(2,1)S(1)} %get-tuple-element.36.u_ref.after_ref, bf16[2,64,180]{2,1,0:T(8,128)(2,1)S(1)} %collective-permute-done.26.row_e, bf16[2,64,180]{2,1,0:T(8,128)(2,1)S(1)} %collective-permute-done.27.row_o, ...), custom_call_target="tpu_custom_call" | custom-call | tf_op jit(solution)/shard_map/squeeze/pallas_call | solution.py:373
  112.7 2.4 %collective-permute-start.33 = (f32[1,180]{1,0:T(1,128)S(1)}, f32[1,180]{1,0:T(1,128)S(1)}, u32[]{:S(2)}, u32[]{:S(2)}) collective-permute-start(f32[1,180]{1,0:T(1,128)S(1)} %add.86.after_ref), channel_id=1, source_target_pairs={{0,6},{1,7},{2,4},{3,5},{4,2},{5,3},{6,0},{7,1},{8,14},{9,15},{10,... | collective-permute-start | bytes 2168 | tf_op jit(solution)/shard_map/ppermute | solution.py:413
  117.1 1.5 collective-permute-done.32
  119.5 2.1 %collective-permute-start.36 = (f32[1,180]{1,0:T(1,128)S(1)}, f32[1,180]{1,0:T(1,128)S(1)}, u32[]{:S(2)}, u32[]{:S(2)}) collective-permute-start(f32[1,180]{1,0:T(1,128)S(1)} %add_add_fusion.1), channel_id=1, source_target_pairs={{0,24},{8,16},{16,8},{24,0},{1,25},{9,17},{17,9},{25,1},{2,26},{10... | collective-permute-start | bytes 2168 | tf_op jit(solution)/shard_map/ppermute | solution.py:413
  121.5 2.3 %collective-permute-start.34 = (f32[1,180]{1,0:T(1,128)S(1)}, f32[1,180]{1,0:T(1,128)S(1)}, u32[]{:S(2)}, u32[]{:S(2)}) collective-permute-start(f32[1,180]{1,0:T(1,128)S(1)} %add_add_fusion.1), channel_id=1, source_target_pairs={{0,8},{8,0},{16,24},{24,16},{1,9},{9,1},{17,25},{25,17},{2,10},{10... | collective-permute-start | bytes 2168 | tf_op jit(solution)/shard_map/ppermute | solution.py:413
  124.5 1.8 %window_attention.11.refs_2_ = f32[16,16,180]{2,1,0:T(8,128)S(1)} custom-call(bf16[16,64,180]{2,1,0:T(8,128)(2,1)S(1)} %get-tuple-element.36.u_ref.after_ref, bf16[3,180,540]{2,1,0:T(8,128)(2,1)S(1)} %copy-done, bf16[3,180,180]{2,1,0:T(8,128)(2,1)S(1)} %copy-done.2, f32[16,64,180]{2,1,0:T(8,128)S(1)} %expand.5.after_ref.exp_ref), custom_call_target="tpu_custom_call" | custom-call | tf_op jit(solution)/shard_map/window_attention/pallas_call | solution.py:373
  126.4 3.8 %feed_forward.5 = (f32[16,64,180]{2,1,0:T(8,128)S(1)}, bf16[16,64,180]{2,1,0:T(8,128)(2,1)S(1)}, bf16[4,64,180]{2,1,0:T(8,128)(2,1)S(1)}, bf16[4,64,180]{2,1,0:T(8,128)(2,1)S(1)}) custom-call(s32[6]{0:T(128)S(1)} %stack.43.flags_ref, f32[16,64,180]{2,1,0:T(8,128)S(1)} %get-tuple-element.35.x_ref, f32[16,64,180]{2,1,0:T(8,128)S(1)} %expand.5.after_ref.exp_ref, ...), custom_call_target="tpu_custom_call" | custom-call | tf_op jit(solution)/shard_map/feed_forward/pallas_call | solution.py:373
  131.3 2.1 %collective-permute-start.38 = (bf16[4,64,180]{2,1,0:T(8,128)(2,1)S(1)}, bf16[4,64,180]{2,1,0:T(8,128)(2,1)S(1)}, u32[]{:S(2)}, u32[]{:S(2)}) collective-permute-start(bf16[4,64,180]{2,1,0:T(8,128)(2,1)S(1)} %get-tuple-element.44), channel_id=1, source_target_pairs={{0,24},{8,16},{16,8},{24,0},{1,25},{9,17},{17,9},{25,1},{2,26},{10... | collective-permute-start | bytes 276488 | tf_op jit(solution)/shard_map/ppermute | solution.py:391
  133.4 1.8 %collective-permute-done.37.row_e = bf16[4,64,180]{2,1,0:T(8,128)(2,1)S(1)} collective-permute-done((bf16[4,64,180]{2,1,0:T(8,128)(2,1)S(1)}, bf16[4,64,180]{2,1,0:T(8,128)(2,1)S(1)}, u32[]{:S(2)}, u32[]{:S(2)}) %collective-permute-start.37) | collective-permute-done | bytes 92192 | tf_op jit(solution)/shard_map/ppermute | solution.py:391
  135.2 2.8 %collective-permute-done.38.row_o = bf16[4,64,180]{2,1,0:T(8,128)(2,1)S(1)} collective-permute-done((bf16[4,64,180]{2,1,0:T(8,128)(2,1)S(1)}, bf16[4,64,180]{2,1,0:T(8,128)(2,1)S(1)}, u32[]{:S(2)}, u32[]{:S(2)}) %collective-permute-start.38) | collective-permute-done | bytes 92192 | tf_op jit(solution)/shard_map/ppermute | solution.py:391
  138.6 4.6 %collective-permute-done.40.col_o = bf16[24,8,180]{2,1,0:T(8,128)(2,1)S(1)} collective-permute-done((bf16[24,8,180]{2,1,0:T(8,128)(2,1)S(1)}, bf16[24,8,180]{2,1,0:T(8,128)(2,1)S(1)}, u32[]{:S(2)}, u32[]{:S(2)}) %collective-permute-start.40) | collective-permute-done | bytes 69152 | tf_op jit(solution)/shard_map/ppermute | solution.py:391
  143.2 11.3 %cross_attention.1.att_ref = f32[16,64,180]{2,1,0:T(8,128)S(1)} custom-call(s32[6]{0:T(128)S(1)} %stack.43.flags_ref, bf16[16,64,180]{2,1,0:T(8,128)(2,1)S(1)} %get-tuple-element.42.u_ref, bf16[4,64,180]{2,1,0:T(8,128)(2,1)S(1)} %collective-permute-done.37.row_e, bf16[4,64,180]{2,1,0:T(8,128)(2,1)S(1)} %collective-permute-done.38.row_o, ...), custom_call_target="tpu_custom_call" | custom-call | tf_op jit(solution)/shard_map/cross_attention/pallas_call | solution.py:373
  154.5 3.0 %last.1 = bf16[16,64,180]{2,1,0:T(8,128)(2,1)} custom-call(f32[16,64,180]{2,1,0:T(8,128)S(1)} %get-tuple-element.41.x_ref, f32[16,64,180]{2,1,0:T(8,128)S(1)} %cross_attention.1.att_ref, bf16[4,180,360]{2,1,0:T(8,128)(2,1)S(1)} %copy-done.3, bf16[4,360,180]{2,1,0:T(8,128)(2,1)S(1)} %copy.13.out_w_ref), custom_call_target="tpu_custom_call" | custom-call | tf_op jit(solution)/shard_map/last/pallas_call | solution.py:373
  (129 shorter events, 25.4 us)
Async XLA Ops:
  0.0 12.2 %copy-start.8 = (bf16[16,64,180]{2,1,0:T(8,128)(2,1)S(1)}, bf16[16,64,180]{2,1,0:T(8,128)(2,1)}, u32[]{:S(2)}) copy-start(bf16[16,64,180]{2,1,0:T(8,128)(2,1)} %x_ref.3) | copy-start | bytes 1105924
  0.9 8.0 %collective-permute-start.1 = (bf16[2,64,180]{2,1,0:T(8,128)(2,1)S(1)}, bf16[2,64,180]{2,1,0:T(8,128)(2,1)S(1)}, u32[]{:S(2)}, u32[]{:S(2)}) collective-permute-start(bf16[2,64,180]{2,1,0:T(8,128)(2,1)S(1)} %get-tuple-element.57), channel_id=1, source_target_pairs={{0,24},{8,16},{16,8},{24,0},{1,25},{9,17},{17,9},{25,1},{2,26},{10... | collective-permute-start | bytes 138248 | tf_op jit(solution)/shard_map/ppermute | solution.py:391
  6.1 4.3 %collective-permute-start = (bf16[2,64,180]{2,1,0:T(8,128)(2,1)S(1)}, bf16[2,64,180]{2,1,0:T(8,128)(2,1)S(1)}, u32[]{:S(2)}, u32[]{:S(2)}) collective-permute-start(bf16[2,64,180]{2,1,0:T(8,128)(2,1)S(1)} %get-tuple-element.58), channel_id=1, source_target_pairs={{0,8},{8,0},{16,24},{24,16},{1,9},{9,1},{17,25},{25,17},{2,10},{10... | collective-permute-start | bytes 138248 | tf_op jit(solution)/shard_map/ppermute | solution.py:391
  7.0 5.5 %copy-start = (bf16[3,180,540]{2,1,0:T(8,128)(2,1)S(1)}, bf16[3,180,540]{2,1,0:T(8,128)(2,1)}, u32[]{:S(2)}) copy-start(bf16[3,180,540]{2,1,0:T(8,128)(2,1)} %qkv_ref.16) | copy-start | bytes 1749604
  10.5 8.2 %collective-permute-start.3 = (bf16[20,2,180]{2,1,0:T(2,128)(2,1)S(1)}, bf16[20,2,180]{2,1,0:T(2,128)(2,1)S(1)}, u32[]{:S(2)}, u32[]{:S(2)}) collective-permute-start(bf16[20,2,180]{2,1,0:T(2,128)(2,1)S(1)} %get-tuple-element.95), channel_id=1, source_target_pairs={{0,7},{1,2},{2,1},{3,4},{4,3},{5,6},{6,5},{7,0},{8,15},{9,10},{10,... | collective-permute-start | bytes 43208 | tf_op jit(solution)/shard_map/ppermute | solution.py:391
  11.5 7.2 %collective-permute-start.2 = (bf16[20,2,180]{2,1,0:T(2,128)(2,1)S(1)}, bf16[20,2,180]{2,1,0:T(2,128)(2,1)S(1)}, u32[]{:S(2)}, u32[]{:S(2)}) collective-permute-start(bf16[20,2,180]{2,1,0:T(2,128)(2,1)S(1)} %get-tuple-element.96), channel_id=1, source_target_pairs={{0,1},{1,0},{2,3},{3,2},{4,5},{5,4},{6,7},{7,6},{8,9},{9,8},{10,11... | collective-permute-start | bytes 43208 | tf_op jit(solution)/shard_map/ppermute | solution.py:391
  16.8 2.5 %copy-start.1 = (bf16[3,9,60,180]{3,2,1,0:T(8,128)(2,1)S(1)}, bf16[3,9,60,180]{3,2,1,0:T(8,128)(2,1)}, u32[]{:S(2)}) copy-start(bf16[3,9,60,180]{3,2,1,0:T(8,128)(2,1)} %w2_ref.11) | copy-start | bytes 1749604
  21.2 15.5 %copy-start.18 = (bf16[4,180,360]{2,0,1:T(4,128)(2,1)S(1)}, bf16[4,180,360]{2,0,1:T(4,128)(2,1)}, u32[]{:S(2)}) copy-start(bf16[4,180,360]{2,0,1:T(4,128)(2,1)} %param.18) | copy-start | bytes 1555204
  24.6 1.2 collective-permute-start.4
  25.8 4.5 %collective-permute-start.7 = (f32[1,180]{1,0:T(1,128)S(1)}, f32[1,180]{1,0:T(1,128)S(1)}, u32[]{:S(2)}, u32[]{:S(2)}) collective-permute-start(f32[1,180]{1,0:T(1,128)S(1)} %add.72.after_ref), channel_id=1, source_target_pairs={{0,6},{1,7},{2,4},{3,5},{4,2},{5,3},{6,0},{7,1},{8,14},{9,15},{10,... | collective-permute-start | bytes 2168 | tf_op jit(solution)/shard_map/ppermute | solution.py:413
  27.2 3.6 %collective-permute-start.6 = (f32[1,180]{1,0:T(1,128)S(1)}, f32[1,180]{1,0:T(1,128)S(1)}, u32[]{:S(2)}, u32[]{:S(2)}) collective-permute-start(f32[1,180]{1,0:T(1,128)S(1)} %add.72.after_ref), channel_id=1, source_target_pairs={{0,4},{1,5},{2,6},{3,7},{4,0},{5,1},{6,2},{7,3},{8,12},{9,13},{10,... | collective-permute-start | bytes 2168 | tf_op jit(solution)/shard_map/ppermute | solution.py:413
  28.7 3.6 %collective-permute-start.5 = (f32[1,180]{1,0:T(1,128)S(1)}, f32[1,180]{1,0:T(1,128)S(1)}, u32[]{:S(2)}, u32[]{:S(2)}) collective-permute-start(f32[1,180]{1,0:T(1,128)S(1)} %add.72.after_ref), channel_id=1, source_target_pairs={{0,2},{1,3},{2,0},{3,1},{4,6},{5,7},{6,4},{7,5},{8,10},{9,11},{10,... | collective-permute-start | bytes 2168 | tf_op jit(solution)/shard_map/ppermute | solution.py:413
  32.3 10.6 %collective-permute-start.10 = (f32[1,180]{1,0:T(1,128)S(1)}, f32[1,180]{1,0:T(1,128)S(1)}, u32[]{:S(2)}, u32[]{:S(2)}) collective-permute-start(f32[1,180]{1,0:T(1,128)S(1)} %add_add_fusion.5), channel_id=1, source_target_pairs={{0,24},{8,16},{16,8},{24,0},{1,25},{9,17},{17,9},{25,1},{2,26},{10... | collective-permute-start | bytes 2168 | tf_op jit(solution)/shard_map/ppermute | solution.py:413
  34.4 8.5 %collective-permute-start.9 = (f32[1,180]{1,0:T(1,128)S(1)}, f32[1,180]{1,0:T(1,128)S(1)}, u32[]{:S(2)}, u32[]{:S(2)}) collective-permute-start(f32[1,180]{1,0:T(1,128)S(1)} %add_add_fusion.5), channel_id=1, source_target_pairs={{0,16},{8,24},{16,0},{24,8},{1,17},{9,25},{17,1},{25,9},{2,18},{10... | collective-permute-start | bytes 2168 | tf_op jit(solution)/shard_map/ppermute | solution.py:413
  34.7 8.2 %collective-permute-start.8 = (f32[1,180]{1,0:T(1,128)S(1)}, f32[1,180]{1,0:T(1,128)S(1)}, u32[]{:S(2)}, u32[]{:S(2)}) collective-permute-start(f32[1,180]{1,0:T(1,128)S(1)} %add_add_fusion.5), channel_id=1, source_target_pairs={{0,8},{8,0},{16,24},{24,16},{1,9},{9,1},{17,25},{25,17},{2,10},{10... | collective-permute-start | bytes 2168 | tf_op jit(solution)/shard_map/ppermute | solution.py:413
  43.0 14.2 %copy-start.5 = (bf16[3,9,180,60]{2,3,1,0:T(8,128)(2,1)S(1)}, bf16[3,9,180,60]{2,3,1,0:T(8,128)(2,1)}, u32[]{:S(2)}) copy-start(bf16[3,9,180,60]{2,3,1,0:T(8,128)(2,1)} %param.14) | copy-start | bytes 1749604
  46.6 4.3 %collective-permute-start.11 = (bf16[2,64,180]{2,1,0:T(8,128)(2,1)S(1)}, bf16[2,64,180]{2,1,0:T(8,128)(2,1)S(1)}, u32[]{:S(2)}, u32[]{:S(2)}) collective-permute-start(bf16[2,64,180]{2,1,0:T(8,128)(2,1)S(1)} %get-tuple-element.29), channel_id=1, source_target_pairs={{0,8},{8,0},{16,24},{24,16},{1,9},{9,1},{17,25},{25,17},{2,10},{10... | collective-permute-start | bytes 138248 | tf_op jit(solution)/shard_map/ppermute | solution.py:391
  46.7 6.2 %collective-permute-start.12 = (bf16[2,64,180]{2,1,0:T(8,128)(2,1)S(1)}, bf16[2,64,180]{2,1,0:T(8,128)(2,1)S(1)}, u32[]{:S(2)}, u32[]{:S(2)}) collective-permute-start(bf16[2,64,180]{2,1,0:T(8,128)(2,1)S(1)} %get-tuple-element.30), channel_id=1, source_target_pairs={{0,24},{8,16},{16,8},{24,0},{1,25},{9,17},{17,9},{25,1},{2,26},{10... | collective-permute-start | bytes 138248 | tf_op jit(solution)/shard_map/ppermute | solution.py:391
  53.0 4.2 %collective-permute-start.14 = (bf16[20,2,180]{2,1,0:T(2,128)(2,1)S(1)}, bf16[20,2,180]{2,1,0:T(2,128)(2,1)S(1)}, u32[]{:S(2)}, u32[]{:S(2)}) collective-permute-start(bf16[20,2,180]{2,1,0:T(2,128)(2,1)S(1)} %get-tuple-element.93), channel_id=1, source_target_pairs={{0,7},{1,2},{2,1},{3,4},{4,3},{5,6},{6,5},{7,0},{8,15},{9,10},{10,... | collective-permute-start | bytes 43208 | tf_op jit(solution)/shard_map/ppermute | solution.py:391
  53.1 4.1 %collective-permute-start.13 = (bf16[20,2,180]{2,1,0:T(2,128)(2,1)S(1)}, bf16[20,2,180]{2,1,0:T(2,128)(2,1)S(1)}, u32[]{:S(2)}, u32[]{:S(2)}) collective-permute-start(bf16[20,2,180]{2,1,0:T(2,128)(2,1)S(1)} %get-tuple-element.94), channel_id=1, source_target_pairs={{0,1},{1,0},{2,3},{3,2},{4,5},{5,4},{6,7},{7,6},{8,9},{9,8},{10,11... | collective-permute-start | bytes 43208 | tf_op jit(solution)/shard_map/ppermute | solution.py:391
  59.4 1.2 collective-permute-start.15
  60.5 5.9 %collective-permute-start.18 = (f32[1,180]{1,0:T(1,128)S(1)}, f32[1,180]{1,0:T(1,128)S(1)}, u32[]{:S(2)}, u32[]{:S(2)}) collective-permute-start(f32[1,180]{1,0:T(1,128)S(1)} %add.79.after_ref), channel_id=1, source_target_pairs={{0,6},{1,7},{2,4},{3,5},{4,2},{5,3},{6,0},{7,1},{8,14},{9,15},{10,... | collective-permute-start | bytes 2168 | tf_op jit(solution)/shard_map/ppermute | solution.py:413
  61.1 5.3 %collective-permute-start.17 = (f32[1,180]{1,0:T(1,128)S(1)}, f32[1,180]{1,0:T(1,128)S(1)}, u32[]{:S(2)}, u32[]{:S(2)}) collective-permute-start(f32[1,180]{1,0:T(1,128)S(1)} %add.79.after_ref), channel_id=1, source_target_pairs={{0,4},{1,5},{2,6},{3,7},{4,0},{5,1},{6,2},{7,3},{8,12},{9,13},{10,... | collective-permute-start | bytes 2168 | tf_op jit(solution)/shard_map/ppermute | solution.py:413
  61.8 4.6 %collective-permute-start.16 = (f32[1,180]{1,0:T(1,128)S(1)}, f32[1,180]{1,0:T(1,128)S(1)}, u32[]{:S(2)}, u32[]{:S(2)}) collective-permute-start(f32[1,180]{1,0:T(1,128)S(1)} %add.79.after_ref), channel_id=1, source_target_pairs={{0,2},{1,3},{2,0},{3,1},{4,6},{5,7},{6,4},{7,5},{8,10},{9,11},{10,... | collective-permute-start | bytes 2168 | tf_op jit(solution)/shard_map/ppermute | solution.py:413
  64.0 7.6 %collective-permute-start.22 = (bf16[8,64,180]{2,1,0:T(8,128)(2,1)S(1)}, bf16[8,64,180]{2,1,0:T(8,128)(2,1)S(1)}, u32[]{:S(2)}, u32[]{:S(2)}) collective-permute-start(bf16[8,64,180]{2,1,0:T(8,128)(2,1)S(1)} %get-tuple-element.33), channel_id=1, source_target_pairs={{0,8},{8,0},{16,24},{24,16},{1,9},{9,1},{17,25},{25,17},{2,10},{10... | collective-permute-start | bytes 552968 | tf_op jit(solution)/shard_map/ppermute | solution.py:391
  64.9 6.8 %collective-permute-start.23 = (bf16[8,64,180]{2,1,0:T(8,128)(2,1)S(1)}, bf16[8,64,180]{2,1,0:T(8,128)(2,1)S(1)}, u32[]{:S(2)}, u32[]{:S(2)}) collective-permute-start(bf16[8,64,180]{2,1,0:T(8,128)(2,1)S(1)} %get-tuple-element.34), channel_id=1, source_target_pairs={{8,16},{16,8},{9,17},{17,9},{10,18},{18,10},{11,19},{19,11},{12,20... | collective-permute-start | bytes 552968 | tf_op jit(solution)/shard_map/ppermute | solution.py:391
  66.4 6.1 %collective-permute-start.21 = (f32[1,180]{1,0:T(1,128)S(1)}, f32[1,180]{1,0:T(1,128)S(1)}, u32[]{:S(2)}, u32[]{:S(2)}) collective-permute-start(f32[1,180]{1,0:T(1,128)S(1)} %add_add_fusion.3), channel_id=1, source_target_pairs={{0,24},{8,16},{16,8},{24,0},{1,25},{9,17},{17,9},{25,1},{2,26},{10... | collective-permute-start | bytes 2168 | tf_op jit(solution)/shard_map/ppermute | solution.py:413
  68.6 6.2 %collective-permute-start.20 = (f32[1,180]{1,0:T(1,128)S(1)}, f32[1,180]{1,0:T(1,128)S(1)}, u32[]{:S(2)}, u32[]{:S(2)}) collective-permute-start(f32[1,180]{1,0:T(1,128)S(1)} %add_add_fusion.3), channel_id=1, source_target_pairs={{0,16},{8,24},{16,0},{24,8},{1,17},{9,25},{17,1},{25,9},{2,18},{10... | collective-permute-start | bytes 2168 | tf_op jit(solution)/shard_map/ppermute | solution.py:413
  71.6 3.6 %collective-permute-start.19 = (f32[1,180]{1,0:T(1,128)S(1)}, f32[1,180]{1,0:T(1,128)S(1)}, u32[]{:S(2)}, u32[]{:S(2)}) collective-permute-start(f32[1,180]{1,0:T(1,128)S(1)} %add_add_fusion.3), channel_id=1, source_target_pairs={{0,8},{8,0},{16,24},{24,16},{1,9},{9,1},{17,25},{25,17},{2,10},{10... | collective-permute-start | bytes 2168 | tf_op jit(solution)/shard_map/ppermute | solution.py:413
  71.8 5.4 %collective-permute-start.25 = (bf16[32,8,180]{2,1,0:T(8,128)(2,1)S(1)}, bf16[32,8,180]{2,1,0:T(8,128)(2,1)S(1)}, u32[]{:S(2)}, u32[]{:S(2)}) collective-permute-start(bf16[32,8,180]{2,1,0:T(8,128)(2,1)S(1)} %get-tuple-element.61), channel_id=1, source_target_pairs={{0,7},{1,2},{2,1},{3,4},{4,3},{5,6},{6,5},{7,0},{8,15},{9,10},{10,... | collective-permute-start | bytes 276488 | tf_op jit(solution)/shard_map/ppermute | solution.py:391
  71.9 5.3 %collective-permute-start.24 = (bf16[32,8,180]{2,1,0:T(8,128)(2,1)S(1)}, bf16[32,8,180]{2,1,0:T(8,128)(2,1)S(1)}, u32[]{:S(2)}, u32[]{:S(2)}) collective-permute-start(bf16[32,8,180]{2,1,0:T(8,128)(2,1)S(1)} %get-tuple-element.62), channel_id=1, source_target_pairs={{0,1},{1,0},{2,3},{3,2},{4,5},{5,4},{6,7},{7,6},{8,9},{9,8},{10,11... | collective-permute-start | bytes 276488 | tf_op jit(solution)/shard_map/ppermute | solution.py:391
  93.2 6.0 %collective-permute-start.26 = (bf16[2,64,180]{2,1,0:T(8,128)(2,1)S(1)}, bf16[2,64,180]{2,1,0:T(8,128)(2,1)S(1)}, u32[]{:S(2)}, u32[]{:S(2)}) collective-permute-start(bf16[2,64,180]{2,1,0:T(8,128)(2,1)S(1)} %get-tuple-element.37), channel_id=1, source_target_pairs={{0,8},{8,0},{16,24},{24,16},{1,9},{9,1},{17,25},{25,17},{2,10},{10... | collective-permute-start | bytes 138248 | tf_op jit(solution)/shard_map/ppermute | solution.py:391
  96.9 6.1 %collective-permute-start.27 = (bf16[2,64,180]{2,1,0:T(8,128)(2,1)S(1)}, bf16[2,64,180]{2,1,0:T(8,128)(2,1)S(1)}, u32[]{:S(2)}, u32[]{:S(2)}) collective-permute-start(bf16[2,64,180]{2,1,0:T(8,128)(2,1)S(1)} %get-tuple-element.38), channel_id=1, source_target_pairs={{0,24},{8,16},{16,8},{24,0},{1,25},{9,17},{17,9},{25,1},{2,26},{10... | collective-permute-start | bytes 138248 | tf_op jit(solution)/shard_map/ppermute | solution.py:391
  103.1 6.1 %collective-permute-start.29 = (bf16[20,2,180]{2,1,0:T(2,128)(2,1)S(1)}, bf16[20,2,180]{2,1,0:T(2,128)(2,1)S(1)}, u32[]{:S(2)}, u32[]{:S(2)}) collective-permute-start(bf16[20,2,180]{2,1,0:T(2,128)(2,1)S(1)} %get-tuple-element.91), channel_id=1, source_target_pairs={{0,7},{1,2},{2,1},{3,4},{4,3},{5,6},{6,5},{7,0},{8,15},{9,10},{10,... | collective-permute-start | bytes 43208 | tf_op jit(solution)/shard_map/ppermute | solution.py:391
  103.2 6.1 %collective-permute-start.28 = (bf16[20,2,180]{2,1,0:T(2,128)(2,1)S(1)}, bf16[20,2,180]{2,1,0:T(2,128)(2,1)S(1)}, u32[]{:S(2)}, u32[]{:S(2)}) collective-permute-start(bf16[20,2,180]{2,1,0:T(2,128)(2,1)S(1)} %get-tuple-element.92), channel_id=1, source_target_pairs={{0,1},{1,0},{2,3},{3,2},{4,5},{5,4},{6,7},{7,6},{8,9},{9,8},{10,11... | collective-permute-start | bytes 43208 | tf_op jit(solution)/shard_map/ppermute | solution.py:391
  111.5 1.2 collective-permute-start.30
  112.7 4.5 %collective-permute-start.33 = (f32[1,180]{1,0:T(1,128)S(1)}, f32[1,180]{1,0:T(1,128)S(1)}, u32[]{:S(2)}, u32[]{:S(2)}) collective-permute-start(f32[1,180]{1,0:T(1,128)S(1)} %add.86.after_ref), channel_id=1, source_target_pairs={{0,6},{1,7},{2,4},{3,5},{4,2},{5,3},{6,0},{7,1},{8,14},{9,15},{10,... | collective-permute-start | bytes 2168 | tf_op jit(solution)/shard_map/ppermute | solution.py:413
  115.1 3.6 %collective-permute-start.32 = (f32[1,180]{1,0:T(1,128)S(1)}, f32[1,180]{1,0:T(1,128)S(1)}, u32[]{:S(2)}, u32[]{:S(2)}) collective-permute-start(f32[1,180]{1,0:T(1,128)S(1)} %add.86.after_ref), channel_id=1, source_target_pairs={{0,4},{1,5},{2,6},{3,7},{4,0},{5,1},{6,2},{7,3},{8,12},{9,13},{10,... | collective-permute-start | bytes 2168 | tf_op jit(solution)/shard_map/ppermute | solution.py:413
  115.9 3.6 %collective-permute-start.31 = (f32[1,180]{1,0:T(1,128)S(1)}, f32[1,180]{1,0:T(1,128)S(1)}, u32[]{:S(2)}, u32[]{:S(2)}) collective-permute-start(f32[1,180]{1,0:T(1,128)S(1)} %add.86.after_ref), channel_id=1, source_target_pairs={{0,2},{1,3},{2,0},{3,1},{4,6},{5,7},{6,4},{7,5},{8,10},{9,11},{10,... | collective-permute-start | bytes 2168 | tf_op jit(solution)/shard_map/ppermute | solution.py:413
  119.5 6.8 %collective-permute-start.36 = (f32[1,180]{1,0:T(1,128)S(1)}, f32[1,180]{1,0:T(1,128)S(1)}, u32[]{:S(2)}, u32[]{:S(2)}) collective-permute-start(f32[1,180]{1,0:T(1,128)S(1)} %add_add_fusion.1), channel_id=1, source_target_pairs={{0,24},{8,16},{16,8},{24,0},{1,25},{9,17},{17,9},{25,1},{2,26},{10... | collective-permute-start | bytes 2168 | tf_op jit(solution)/shard_map/ppermute | solution.py:413
  121.5 4.8 %collective-permute-start.35 = (f32[1,180]{1,0:T(1,128)S(1)}, f32[1,180]{1,0:T(1,128)S(1)}, u32[]{:S(2)}, u32[]{:S(2)}) collective-permute-start(f32[1,180]{1,0:T(1,128)S(1)} %add_add_fusion.1), channel_id=1, source_target_pairs={{0,16},{8,24},{16,0},{24,8},{1,17},{9,25},{17,1},{25,9},{2,18},{10... | collective-permute-start | bytes 2168 | tf_op jit(solution)/shard_map/ppermute | solution.py:413
  121.5 4.8 %collective-permute-start.34 = (f32[1,180]{1,0:T(1,128)S(1)}, f32[1,180]{1,0:T(1,128)S(1)}, u32[]{:S(2)}, u32[]{:S(2)}) collective-permute-start(f32[1,180]{1,0:T(1,128)S(1)} %add_add_fusion.1), channel_id=1, source_target_pairs={{0,8},{8,0},{16,24},{24,16},{1,9},{9,1},{17,25},{25,17},{2,10},{10... | collective-permute-start | bytes 2168 | tf_op jit(solution)/shard_map/ppermute | solution.py:413
  130.1 5.1 %collective-permute-start.37 = (bf16[4,64,180]{2,1,0:T(8,128)(2,1)S(1)}, bf16[4,64,180]{2,1,0:T(8,128)(2,1)S(1)}, u32[]{:S(2)}, u32[]{:S(2)}) collective-permute-start(bf16[4,64,180]{2,1,0:T(8,128)(2,1)S(1)} %get-tuple-element.43), channel_id=1, source_target_pairs={{0,8},{8,0},{16,24},{24,16},{1,9},{9,1},{17,25},{25,17},{2,10},{10... | collective-permute-start | bytes 276488 | tf_op jit(solution)/shard_map/ppermute | solution.py:391
  131.3 6.8 %collective-permute-start.38 = (bf16[4,64,180]{2,1,0:T(8,128)(2,1)S(1)}, bf16[4,64,180]{2,1,0:T(8,128)(2,1)S(1)}, u32[]{:S(2)}, u32[]{:S(2)}) collective-permute-start(bf16[4,64,180]{2,1,0:T(8,128)(2,1)S(1)} %get-tuple-element.44), channel_id=1, source_target_pairs={{0,24},{8,16},{16,8},{24,0},{1,25},{9,17},{17,9},{25,1},{2,26},{10... | collective-permute-start | bytes 276488 | tf_op jit(solution)/shard_map/ppermute | solution.py:391
  138.1 5.1 %copy-start.12 = (bf16[180,540]{1,0:T(8,128)(2,1)S(1)}, bf16[180,540]{1,0:T(8,128)(2,1)}, u32[]{:S(2)}) copy-start(bf16[180,540]{1,0:T(8,128)(2,1)} %qkv_ref.17) | copy-start | bytes 583204
  138.1 5.1 %copy-start.15 = (bf16[180,180]{1,0:T(8,128)(2,1)S(1)}, bf16[180,180]{1,0:T(8,128)(2,1)}, u32[]{:S(2)}) copy-start(bf16[180,180]{1,0:T(8,128)(2,1)} %proj_ref.17) | copy-start | bytes 194404
  138.2 5.0 %collective-permute-start.40 = (bf16[24,8,180]{2,1,0:T(8,128)(2,1)S(1)}, bf16[24,8,180]{2,1,0:T(8,128)(2,1)S(1)}, u32[]{:S(2)}, u32[]{:S(2)}) collective-permute-start(bf16[24,8,180]{2,1,0:T(8,128)(2,1)S(1)} %get-tuple-element.67), channel_id=1, source_target_pairs={{0,7},{1,2},{2,1},{3,4},{4,3},{5,6},{6,5},{7,0},{8,15},{9,10},{10,... | collective-permute-start | bytes 207368 | tf_op jit(solution)/shard_map/ppermute | solution.py:391
  138.2 4.9 %collective-permute-start.39 = (bf16[24,8,180]{2,1,0:T(8,128)(2,1)S(1)}, bf16[24,8,180]{2,1,0:T(8,128)(2,1)S(1)}, u32[]{:S(2)}, u32[]{:S(2)}) collective-permute-start(bf16[24,8,180]{2,1,0:T(8,128)(2,1)S(1)} %get-tuple-element.68), channel_id=1, source_target_pairs={{0,1},{1,0},{2,3},{3,2},{4,5},{5,4},{6,7},{7,6},{8,9},{9,8},{10,11... | collective-permute-start | bytes 207368 | tf_op jit(solution)/shard_map/ppermute | solution.py:391
  (12 other events, 16.7 us)
